TPU v7x, 32 devices: a whole 2x2x4 slice. The times are simulated.
32 devices in a mesh: tiles: 2 (over y), pat: 16 (over z, x, core).
Axes of the slice: x: 2, y: 2, z: 4, core: 2. Of those that a mesh axis runs over, the one named last changes fastest.
Arguments:
- slab_phase: float32 [6, 1024, 1024], P('tiles', 'pat'), parts along dimension 0, may hold values from -2 to 2
- pupil_phase: float32 [1024, 1024], P('pat'), may hold values from -5 to 5
- pupil_mask: int32 [1024, 1024], P('pat'), may hold values from 0 to 1, as said below
- led_code: int32 [4, 2], replicated, may hold values from 0 to 1, as said below
- led_freq: int32 [2, 2], replicated, may hold values from -32 to 32
- measured: int32 [8, 1024, 1024], P('tiles', 'pat'), parts along dimension 0, may hold values from 1 to 2048
Outputs:
- phase_grad: float32 [6, 1024, 1024], P('tiles', 'pat'), parts along dimension 0
There are 2 independent parts, one for each index of `tiles`. A program takes and returns all parts, laid end to end along the dimension named above; an argument that names none is the same for every part. Nothing has to cross between parts.
Inputs may be any that keep to these rules, and one draw needn't show every extreme that they name: `pupil_mask`: 1 at every frequency pair with freq(u)^2 + freq(v)^2 <= 9216, 0 where it is >= 16384, either value between. `led_code`: pattern p always has LED p mod 2 switched on.
All inputs are finite; a program needn't handle non-finite values.
Results may differ from a plain program's by a relative error of at most 0.0003.
Values sent between devices are 32-bit elements; how exact they have to be, the bound alone decides.
A program may use at most 128 MiB of HBM per device.

v0:
```python
import functools
import math
import types

import jax
import jax.numpy as jnp
import numpy as np
from jax import lax
from jax.experimental import pallas as pl
from jax.experimental.pallas import tpu as pltpu
from jax.sharding import PartitionSpec as P

spread_rate = 0.3
highest = lax.Precision.HIGHEST


def frequency(grid_index, grid_size):
    return (grid_index + grid_size // 2) % grid_size - grid_size // 2


def complex_times(values, factor):
    real_part = values[0] * factor[0] - values[1] * factor[1]
    imag_part = values[0] * factor[1] + values[1] * factor[0]
    return jnp.stack([real_part, imag_part])


def dft_block(length, direction, norm_factor):
    grid_index = jnp.arange(length, dtype=jnp.int32)
    angles = (grid_index[:, None] * grid_index[None, :] % length).astype(jnp.float32) * (
        2.0 * math.pi / length
    )
    cosine = jnp.cos(angles) * norm_factor
    signed_sine = direction * jnp.sin(angles) * norm_factor
    real_rows = jnp.stack([cosine, signed_sine], 1)
    imag_rows = jnp.stack([-signed_sine, cosine], 1)
    return jnp.stack([real_rows, imag_rows], 0)


def twiddle_table(short_size, long_size, grid_size, direction):
    short_index = jnp.arange(short_size, dtype=jnp.int32)
    long_index = jnp.arange(long_size, dtype=jnp.int32)
    angles = (short_index[:, None] * long_index[None, :] % grid_size).astype(jnp.float32) * (
        2.0 * math.pi / grid_size
    )
    return jnp.stack([jnp.cos(angles), direction * jnp.sin(angles)])


def table_set(col_count, dev_count, grid_size, direction):
    short_table = dft_block(col_count, direction, 1.0)
    long_table = dft_block(dev_count, direction, 1.0 / math.sqrt(grid_size))
    return (short_table, long_table, twiddle_table(col_count, dev_count, grid_size, direction))


def to_fourier(wave_field, tables, dev_count):
    short_table, long_table, twiddles = tables
    led_count = wave_field.shape[1]
    row_count = wave_field.shape[2]
    grid_size = wave_field.shape[3]
    col_count = grid_size // dev_count
    shaped = wave_field.reshape(2, led_count, row_count, col_count, dev_count)
    sectioned = jnp.einsum("zlrmq,zmwc->wlrcq", shaped, short_table, precision=highest)
    sectioned = complex_times(sectioned, twiddles)
    outgoing = jnp.einsum("wlrcq,wqvd->dvlcr", sectioned, long_table, precision=highest)
    incoming = lax.all_to_all(
        outgoing.reshape(dev_count, -1), "pat", split_axis=0, concat_axis=0, tiled=True
    )
    incoming = incoming.reshape(dev_count, 2, led_count, col_count, row_count)
    sectioned = jnp.einsum("swlcr,wsvj->vlcrj", incoming, long_table, precision=highest)
    sectioned = complex_times(sectioned, twiddles)
    sectioned = jnp.einsum("wlcrj,wrvh->vlchj", sectioned, short_table, precision=highest)
    return sectioned.reshape(2, led_count, col_count, grid_size)


def to_space(spectrum, tables, dev_count):
    short_table, long_table, twiddles = tables
    led_count = spectrum.shape[1]
    col_count = spectrum.shape[2]
    grid_size = spectrum.shape[3]
    row_count = grid_size // dev_count
    shaped = spectrum.reshape(2, led_count, col_count, row_count, dev_count)
    sectioned = jnp.einsum("zlcmq,zmwr->wlcrq", shaped, short_table, precision=highest)
    sectioned = complex_times(sectioned, twiddles)
    outgoing = jnp.einsum("wlcrq,wqvd->dvlcr", sectioned, long_table, precision=highest)
    incoming = lax.all_to_all(
        outgoing.reshape(dev_count, -1), "pat", split_axis=0, concat_axis=0, tiled=True
    )
    incoming = incoming.reshape(dev_count, 2, led_count, col_count, row_count)
    sectioned = jnp.einsum("swlcr,wsvj->vlrcj", incoming, long_table, precision=highest)
    sectioned = complex_times(sectioned, twiddles)
    sectioned = jnp.einsum("wlrcj,wcvh->vlrhj", sectioned, short_table, precision=highest)
    return sectioned.reshape(2, led_count, row_count, grid_size)


def plain_body(slab_phase, pupil_phase, pupil_mask, led_code, led_freq, measured):
    dev_count = lax.axis_size("pat")
    position = lax.axis_index("pat")
    slab_count, row_count, grid_size = slab_phase.shape
    col_count = grid_size // dev_count
    pattern_count, led_count = led_code.shape
    area = float(grid_size * grid_size)
    forward_set = table_set(col_count, dev_count, grid_size, -1.0)
    inverse_set = table_set(col_count, dev_count, grid_size, 1.0)
    conjugate = jnp.array([1.0, -1.0], jnp.float32)[:, None, None]
    col_freq = frequency(position * col_count + jnp.arange(col_count, dtype=jnp.int32), grid_size)
    row_freq = frequency(jnp.arange(grid_size, dtype=jnp.int32), grid_size)
    radius = col_freq[:, None] * col_freq[:, None] + row_freq[None, :] * row_freq[None, :]
    cutoff = grid_size // 2 * (grid_size // 2)
    inside = radius <= cutoff
    height = jnp.sqrt(jnp.maximum(cutoff - radius, 0).astype(jnp.float32))
    phase_shift = spread_rate * (height - grid_size // 2)
    propagator = jnp.stack(
        [jnp.where(inside, jnp.cos(phase_shift), 0.0), jnp.where(inside, jnp.sin(phase_shift), 0.0)]
    )
    opening = pupil_mask.astype(jnp.float32)
    pupil = jnp.stack([opening * jnp.cos(pupil_phase), opening * jnp.sin(pupil_phase)])
    propagator_conj = propagator * conjugate
    pupil_conj = pupil * conjugate
    row_index = position * row_count + jnp.arange(row_count, dtype=jnp.int32)
    col_index = jnp.arange(grid_size, dtype=jnp.int32)
    tilt_index = (
        led_freq[:, 0][:, None, None] * row_index[None, :, None]
        + led_freq[:, 1][:, None, None] * col_index[None, None, :]
    ) % grid_size
    tilt_angle = tilt_index.astype(jnp.float32) * (2.0 * math.pi / grid_size)
    illumination = jnp.stack([jnp.cos(tilt_angle), jnp.sin(tilt_angle)])
    transmission = jnp.stack([jnp.cos(slab_phase), jnp.sin(slab_phase)])
    group_count = 1
    group_size = led_count // group_count
    wave_groups = [illumination]
    passed_groups = []
    for slab_index in range(slab_count):
        factor = transmission[:, slab_index]
        passed = [complex_times(wave_field, factor) for wave_field in wave_groups]
        passed_groups.append(passed)
        spectral_factor = propagator if slab_index < slab_count - 1 else pupil
        wave_groups = [
            to_space(
                complex_times(to_fourier(passed_field, forward_set, dev_count), spectral_factor),
                inverse_set,
                dev_count,
            )
            for passed_field in passed
        ]
    camera = wave_groups[0]
    led_power = camera[0] * camera[0] + camera[1] * camera[1]
    code_float = led_code.astype(jnp.float32)
    pattern_power = jnp.dot(
        code_float, led_power.reshape(led_count, -1), precision=highest
    ).reshape(pattern_count, row_count, grid_size)
    counts = measured.astype(jnp.float32)
    power_sum, count_sum = lax.psum(
        (jnp.sum(pattern_power, axis=(1, 2)), jnp.sum(counts, axis=(1, 2))), "pat"
    )
    mean_power = power_sum / area
    mean_count = count_sum / area
    relative = pattern_power / mean_power[:, None, None]
    misfit = relative - counts / mean_count[:, None, None]
    coupling = lax.psum(jnp.sum(misfit * relative, axis=(1, 2)), "pat") / area
    pattern_weight = (misfit - coupling[:, None, None]) / mean_power[:, None, None]
    led_weight = jnp.dot(
        code_float.T, pattern_weight.reshape(pattern_count, -1), precision=highest
    ).reshape(led_count, row_count, grid_size)
    camera_adjoint = 2.0 * led_weight[None] * camera
    adjoint_groups = [camera_adjoint]
    gradients = [None] * slab_count
    for slab_index in range(slab_count - 1, -1, -1):
        spectral_factor = pupil_conj if slab_index == slab_count - 1 else propagator_conj
        back_groups = [
            to_space(
                complex_times(to_fourier(adjoint_field, forward_set, dev_count), spectral_factor),
                inverse_set,
                dev_count,
            )
            for adjoint_field in adjoint_groups
        ]
        gradient = jnp.zeros((row_count, grid_size), jnp.float32)
        for passed_field, back_field in zip(passed_groups[slab_index], back_groups):
            gradient = jnp.sum(
                passed_field[0] * back_field[1] - passed_field[1] * back_field[0], axis=0
            )
        gradients[slab_index] = gradient
        if slab_index > 0:
            release = transmission[:, slab_index] * conjugate
            adjoint_groups = [complex_times(back_field, release) for back_field in back_groups]
    return jnp.stack(gradients)


class Names(types.SimpleNamespace):
    pass


pupil_radius = 128
lanes = 128
f32 = jnp.float32
bf16 = jnp.bfloat16


def halves(table):
    table32 = np.asarray(table, np.float32)
    high = table32.astype(bf16)
    low = (table32 - high.astype(np.float32)).astype(bf16)
    return np.stack([high, low])


def row_tables(size, block, band_block):
    quarter = size // 4
    pos = np.arange(quarter)
    angle = 2.0 * np.pi * ((pos[:, None] * pos[None, :]) % quarter) / quarter
    cosine = np.cos(angle) / math.sqrt(size)
    sine = np.sin(angle) / math.sqrt(size)

    def forward(freqs, width):
        parts = []
        for first in range(0, len(freqs), width):
            pick = freqs[first : first + width] % quarter
            left = np.concatenate([cosine[:, pick], sine[:, pick]], 0)
            right = np.concatenate([-sine[:, pick], cosine[:, pick]], 0)
            parts.append(np.concatenate([left, right], 1))
        return np.concatenate(parts, 1)

    full = forward(pos, block)
    reach = pupil_radius // 4
    band = forward(np.arange(-reach, reach), band_block)
    theta = 2.0 * np.pi * (np.arange(4)[:, None] * pos[None, :]) / size
    twiddle = np.concatenate([np.cos(theta), np.sin(theta)], 0).astype(np.float32)
    return Names(
        full=jnp.asarray(halves(full)),
        full_inv=jnp.asarray(halves(full.T)),
        band=jnp.asarray(halves(band)),
        band_inv=jnp.asarray(halves(band.T)),
        twiddle=jnp.asarray(twiddle),
    )


def col_tables(size):
    quarter = size // 4
    pos = np.arange(quarter)
    angle = 2.0 * np.pi * ((pos[:, None] * pos[None, :]) % quarter) / quarter
    both = np.concatenate([np.cos(angle), np.sin(angle)], 0) / math.sqrt(size)
    theta = 2.0 * np.pi * (np.arange(1, 4)[:, None] * pos[None, :]) / size
    twiddle = np.stack([np.cos(theta), np.sin(theta)]).astype(np.float32)
    twiddle = np.ascontiguousarray(np.broadcast_to(twiddle[..., None], twiddle.shape + (lanes,)))
    freqs = np.arange(-pupil_radius, pupil_radius)
    angle = 2.0 * np.pi * ((np.arange(size)[:, None] * freqs[None, :]) % size) / size
    cosine = np.cos(angle) / math.sqrt(size)
    sine = np.sin(angle) / math.sqrt(size)
    band = halves(np.concatenate([cosine, sine], 1))
    band_inv = halves(np.concatenate([cosine.T, sine.T], 1))
    return Names(both=halves(both), twiddle=twiddle, band=band, band_inv=band_inv)


def split(value):
    high = value.astype(bf16)
    return high, (value - high.astype(f32)).astype(bf16)


def dot3(left, right):
    def dot(a, b):
        return jnp.dot(a, b, preferred_element_type=f32)

    return dot(left[0], right[0]) + (dot(left[0], right[1]) + dot(left[1], right[0]))


def turn(value):
    rolled = pltpu.roll(value, lanes // 2, 1)
    lane = lax.broadcasted_iota(jnp.int32, value.shape, 1)
    return jnp.where(lane < lanes // 2, rolled, -rolled)


def partner(me, step, devs):
    return lax.rem(me + step, devs)


def greet(devs):
    me = lax.axis_index("pat")
    barrier = pltpu.get_barrier_semaphore()

    def signal(step, carry):
        pl.semaphore_signal(
            barrier, inc=1, device_id=dict(pat=partner(me, step, devs)),
            device_id_type=pl.DeviceIdType.MESH,
        )
        return carry

    lax.fori_loop(1, devs, signal, 0)
    return me, barrier


def view(ref, at, part):
    return ref.at[at] if part is None else ref.at[at, part]


def remote(ref, me, dest, part, land):
    block = ref.stage if ref.same else view(ref.stage, dest, part)
    row = 0 if part is None else part
    return pltpu.make_async_remote_copy(
        src_ref=block, dst_ref=view(ref.y, land, part), send_sem=ref.sent.at[row, dest],
        recv_sem=ref.got.at[row, land], device_id=dict(pat=dest),
        device_id_type=pl.DeviceIdType.MESH,
    )


def send(ref, me, dest, part=None):
    @pl.when(dest != me)
    def _():
        remote(ref, me, dest, part, me).start()

    @pl.when(dest == me)
    def _():
        keep(ref, me, part).start()


def groups(me, per):
    z = me // per
    return [lax.rem(z + 2, 4), 3 - z, z + 1 - 2 * lax.rem(z, 2), z]


def send_all(ref, me, devs, part=None):
    per = devs // 4
    for j in groups(me, per):

        def share(q, carry):
            send(ref, me, per * j + lax.rem(me + q, per), part)
            return carry

        lax.fori_loop(0, per, share, 0)


def keep(ref, me, part):
    block = ref.stage if ref.same else view(ref.stage, me, part)
    return pltpu.make_async_copy(block, view(ref.y, me, part), ref.kept.at[0 if part is None else part])


def finish(ref, me, devs, parts=(None,)):
    for part in parts:

        def settle(step, carry):
            other = partner(me, step, devs)
            remote(ref, me, other, part, other).wait()
            return carry

        keep(ref, me, part).wait()
        lax.fori_loop(1, devs, settle, 0)


def comm_scratch(stage_shape, devs, parts=1):
    return [
        pltpu.VMEM(stage_shape, f32),
        pltpu.SemaphoreType.DMA((parts, devs)),
        pltpu.SemaphoreType.DMA((parts, devs)),
        pltpu.SemaphoreType.DMA((parts,)),
    ]


def comm_params(channel):
    return pltpu.CompilerParams(collective_id=channel, has_side_effects=True)


anywhere = pl.BlockSpec(memory_space=pl.ANY)


def row_spread(blocks, twiddle_ref):
    (r0, i0), (r1, i1), (r2, i2), (r3, i3) = blocks
    sr, si, tr, ti = r0 + r2, i0 + i2, r1 + r3, i1 + i3
    dr, di, er, ei = r0 - r2, i0 - i2, r1 - r3, i1 - i3
    mixed = [(sr + tr, si + ti), (dr + ei, di - er), (sr - tr, si - ti), (dr - ei, di + er)]
    out = [mixed[0]]
    for j in range(1, 4):
        cosine, sine = twiddle_ref[j : j + 1, :], twiddle_ref[4 + j : 5 + j, :]
        re, im = mixed[j]
        out.append((re * cosine + im * sine, im * cosine - re * sine))
    return out


def row_gather(parts, twiddle_ref):
    g = [parts[0]]
    for j in range(1, 4):
        cosine, sine = twiddle_ref[j : j + 1, :], twiddle_ref[4 + j : 5 + j, :]
        re, im = parts[j]
        g.append((re * cosine - im * sine, im * cosine + re * sine))
    (r0, i0), (r1, i1), (r2, i2), (r3, i3) = g
    sr, si, tr, ti = r0 + r2, i0 + i2, r1 + r3, i1 + i3
    dr, di, er, ei = r0 - r2, i0 - i2, r1 - r3, i1 - i3
    return [(sr + tr, si + ti), (dr - ei, di + er), (sr - tr, si - ti), (dr + ei, di - er)]


def row_kernel(spec, *refs):
    ref = Names(**dict(zip(spec.names, refs)), same=spec.kind == "stats")
    sends = spec.kind != "leave"
    if sends:
        me, barrier = greet(spec.devs)
    count, rows, quarter = spec.count, spec.rows, spec.quarter
    devs = spec.devs
    per = devs // 4
    step = 16
    total = count * rows
    hi, lo, zs, twiddle = ref.hi, ref.lo, ref.zs, ref.twiddle
    source = spec.source
    if source == "full":
        for j in range(4):
            for q in range(per):
                block = ref.x[per * j + q].reshape(total, lanes)
                high, low = split(block)
                hi[j, :total, q * lanes : (q + 1) * lanes] = high
                lo[j, :total, q * lanes : (q + 1) * lanes] = low
        for j in range(4):
            left = (hi[j, :total, :], lo[j, :total, :])
            zs[j, :total, :] = dot3(left, (ref.inv[0], ref.inv[1]))
    elif source == "band":
        for j in range(4):
            block = ref.x[per * j : per * (j + 1)].reshape(-1, total)
            zs[j, :total, :] = dot3(split(block.T), (ref.inv[0], ref.inv[1]))
    kind = spec.kind
    if kind == "stats":
        stats = [jnp.zeros((8, lanes), f32) for _ in range(spec.stat_rows)]
    if kind == "weigh":
        sums = jnp.sum(ref.stats[...], 0)
        sums = jnp.sum(sums, 1, keepdims=True)
        code = [[ref.code[p, l].astype(f32) for l in range(count)] for p in range(spec.patterns)]
        area = spec.area
        power_mean, count_mean, couple = [], [], []
        base = count + count * (count + 1) // 2
        for p in range(spec.patterns):
            mean = sum(sums[l : l + 1] * code[p][l] for l in range(count)) / area
            mean_count = sums[base + spec.patterns * count + p :][:1] / area
            square = 0.0
            at = count
            for l in range(count):
                for m in range(l, count):
                    factor = 1.0 if l == m else 2.0
                    square = square + (factor * code[p][l] * code[p][m]) * sums[at : at + 1]
                    at += 1
            cross = sum(code[p][l] * sums[base + p * count + l :][:1] for l in range(count))
            power_mean.append(mean)
            count_mean.append(mean_count)
            couple.append((square / mean / mean - cross / mean_count / mean) / area)

    def fold(value):
        total_rows = value[:8]
        for k in range(1, value.shape[0] // 8):
            total_rows = total_rows + value[8 * k : 8 * k + 8]
        out = total_rows[:, :lanes]
        for k in range(1, value.shape[1] // lanes):
            out = out + total_rows[:, lanes * k : lanes * (k + 1)]
        return out

    def chunk(i, carry):
        base_row = pl.multiple_of(i * step, step)
        here = pl.ds(base_row, step)
        fields = []
        for l in range(count):
            at = pl.ds(pl.multiple_of(l * rows + base_row, step), step)
            if source in ("full", "band"):
                parts = [(zs[j, at, :quarter], zs[j, at, quarter:]) for j in range(4)]
                fields.append(row_gather(parts, twiddle))
        cut = [slice(a * quarter, (a + 1) * quarter) for a in range(4)]

        def tilt(l, a, value, sign):
            rc, rs = ref.tilt_r[2 * l, here, :], ref.tilt_r[2 * l + 1, here, :]
            cc, cs = ref.tilt_c[2 * l : 2 * l + 1, cut[a]], ref.tilt_c[2 * l + 1 : 2 * l + 2, cut[a]]
            wide = jnp.concatenate([rc] * (quarter // lanes), 1), jnp.concatenate([rs] * (quarter // lanes), 1)
            er = wide[0] * cc - wide[1] * cs
            ei = sign * (wide[0] * cs + wide[1] * cc)
            re, im = value
            return re * er - im * ei, re * ei + im * er

        outgoing = []
        if kind == "enter":
            outgoing = [[]]
            for c in cut:
                phase = ref.slab[0, here, c]
                cosine, sine = jnp.cos(phase), jnp.sin(phase)
                ref.tr0[0, here, c] = cosine
                ref.tr0[1, here, c] = sine
                outgoing[0].append((cosine, sine))
        elif kind == "forward" or kind == "forward_band":
            for l in range(count):
                at = pl.ds(pl.multiple_of(l * rows + base_row, step), step)
                blocks = []
                for a, c in enumerate(cut):
                    tr, ti = ref.tr[0, here, c], ref.tr[1, here, c]
                    re, im = fields[l][a]
                    re, im = re * tr - im * ti, re * ti + im * tr
                    ref.passed[0, at, c] = re
                    ref.passed[1, at, c] = im
                    blocks.append((re, im) if kind == "forward" else tilt(l, a, (re, im), 1.0))
                outgoing.append(blocks)
        elif kind == "stats":
            adds = [0.0] * spec.stat_rows
            for a, c in enumerate(cut):
                power = []
                for l in range(count):
                    at = pl.ds(pl.multiple_of(l * rows + base_row, step), step)
                    re, im = fields[l][a]
                    ref.passed[0, at, c] = re
                    ref.passed[1, at, c] = im
                    power.append(re * re + im * im)
                values = list(power)
                for l in range(count):
                    for m in range(l, count):
                        values.append(power[l] * power[m])
                seen = [ref.measured[p, here, c].astype(f32) for p in range(spec.patterns)]
                for p in range(spec.patterns):
                    for l in range(count):
                        values.append(seen[p] * power[l])
                values += seen
                for k, value in enumerate(values):
                    adds[k] = adds[k] + fold(value)
            return tuple(x + y for x, y in zip(carry, adds))
        elif kind == "weigh":
            outgoing = [[] for _ in range(count)]
            for a, c in enumerate(cut):
                camera, power = [], []
                for l in range(count):
                    at = pl.ds(pl.multiple_of(l * rows + base_row, step), step)
                    re, im = ref.passed[0, at, c], ref.passed[1, at, c]
                    camera.append((re, im))
                    power.append(re * re + im * im)
                weight = [0.0] * count
                for p in range(spec.patterns):
                    lit = sum(code[p][l] * power[l] for l in range(count))
                    seen = ref.measured[p, here, c].astype(f32)
                    misfit = lit * (1.0 / power_mean[p]) - seen * (1.0 / count_mean[p])
                    pull = (misfit - couple[p]) * (1.0 / power_mean[p])
                    for l in range(count):
                        weight[l] = weight[l] + code[p][l] * pull
                for l in range(count):
                    scale = 2.0 * weight[l]
                    outgoing[l].append((scale * camera[l][0], scale * camera[l][1]))
        elif kind == "back" or kind == "back_band":
            grads = [0.0] * 4
            for l in range(count):
                at = pl.ds(pl.multiple_of(l * rows + base_row, step), step)
                blocks = []
                for a, c in enumerate(cut):
                    re, im = fields[l][a]
                    if kind == "back_band":
                        re, im = tilt(l, a, (re, im), -1.0)
                    pr, pi = ref.passed[0, at, c], ref.passed[1, at, c]
                    grads[a] = grads[a] + (pr * im - pi * re)
                    tr, ti = ref.tr[0, here, c], ref.tr[1, here, c]
                    blocks.append((re * tr + im * ti, im * tr - re * ti))
                outgoing.append(blocks)
            for a, c in enumerate(cut):
                ref.grad[here, c] = grads[a]
        elif kind == "leave":
            for a, c in enumerate(cut):
                tr, ti = ref.tr[0, here, c], ref.tr[1, here, c]
                re, im = fields[0][a]
                ref.grad[here, c] = tr * im - ti * re
        for l, blocks in enumerate(outgoing):
            at = pl.ds(pl.multiple_of(l * rows + base_row, step), step)
            for j, (re, im) in enumerate(row_spread(blocks, twiddle)):
                high, low = split(re)
                hi[j, at, :quarter] = high
                lo[j, at, :quarter] = low
                high, low = split(im)
                hi[j, at, quarter:] = high
                lo[j, at, quarter:] = low
        return carry

    if kind == "stats":
        stats = lax.fori_loop(0, rows // step, chunk, tuple(stats))
        packed = [jnp.sum(row, 0, keepdims=True) for row in stats]
        packed.append(jnp.zeros((ref.stage.shape[0] - len(packed), lanes), f32))
        packed = jnp.concatenate(packed, 0)
        ref.stage[...] = packed
        pl.semaphore_wait(barrier, devs - 1)
        send_all(ref, me, devs)
        finish(ref, me, devs)
        return
    lax.fori_loop(0, rows // step, chunk, 0)
    if not sends:
        return
    pl.semaphore_wait(barrier, devs - 1)

    def emit(j):
        y = dot3((hi[j, :total, :], lo[j, :total, :]), (ref.fwd[0], ref.fwd[1]))
        if spec.target == "full":
            for q in range(per):
                ref.stage[per * j + q] = y[:, q * lanes : (q + 1) * lanes].reshape(count, rows, lanes)
        else:
            flipped = y.T
            deep = flipped.shape[0] // per
            for q in range(per):
                ref.stage[per * j + q] = flipped[q * deep : (q + 1) * deep]
        for q in range(per):
            send(ref, me, per * j + lax.rem(me + q, per))

    for j in groups(me, per):
        emit(j)
    if kind == "enter":
        pupil_out(spec, ref, me)
        prepare(spec, ref, me)
        pupil_in(spec, ref, me)
    finish(ref, me, devs)


def pupil_copy(spec, ref, j, dest):
    return pltpu.make_async_remote_copy(
        src_ref=ref.own.at[j], dst_ref=ref.pupil, send_sem=ref.psent.at[j], recv_sem=ref.pgot,
        device_id=dict(pat=dest), device_id_type=pl.DeviceIdType.MESH,
    )


def pupil_out(spec, ref, me):
    per = spec.devs // 4
    for q in range(per):

        @pl.when(me == spec.owners[q])
        def _():
            for j in range(4):
                pupil_copy(spec, ref, j, per * j + q).start()


def pupil_in(spec, ref, me):
    per = spec.devs // 4
    pupil_copy(spec, ref, 0, partner(me, 1, spec.devs)).wait_recv()
    for q in range(per):

        @pl.when(me == spec.owners[q])
        def _():
            for j in range(4):
                pupil_copy(spec, ref, j, per * j + q).wait_send()


def prepare(spec, ref, me):
    size, quarter = 4 * spec.quarter, spec.quarter
    per, half, step = spec.devs // 4, lanes // 2, 16
    cutoff = size // 2 * (size // 2)

    def phases(i, carry):
        here = pl.ds(pl.multiple_of(i * step, step), step)
        for s, out in ((1, ref.tr1), (2, ref.tr2)):
            phase = ref.slab[s, here, :]
            out[0, here, :] = jnp.cos(phase)
            out[1, here, :] = jnp.sin(phase)
        return carry

    lax.fori_loop(0, spec.rows // step, phases, 0)

    def centred(index):
        return jnp.where(index >= size // 2, index - size, index)

    def spectrum(i, carry):
        here = pl.ds(pl.multiple_of(i * step, step), step)
        row = lax.broadcasted_iota(jnp.int32, (step, lanes), 0) + i * step
        lane = lax.broadcasted_iota(jnp.int32, (step, lanes), 1)
        lane = jnp.where(lane < half, lane, lane - half)
        col = 4 * (lax.rem(me, per) * half + lane) + me // per
        for l in range(spec.leds):
            v = centred(col + ref.freq[l, 1])
            for j in range(4):
                u = centred(4 * row + j + ref.freq[l, 0])
                radius = u * u + v * v
                inside = radius <= cutoff
                height = jnp.sqrt(jnp.maximum(cutoff - radius, 0).astype(f32))
                shift = spread_rate * (height - float(size // 2))
                ref.prop[0, l, j, here, :] = jnp.where(inside, jnp.cos(shift), 0.0)
                ref.prop[1, l, j, here, :] = jnp.where(inside, jnp.sin(shift), 0.0)
        return carry

    lax.fori_loop(0, quarter // step, spectrum, 0)


def run_rows(channel, kind, source, target, dims, inputs, outputs):
    spec = Names(**vars(dims), kind=kind, source=source, target=target)
    count = spec.count
    total = count * spec.rows
    wide = 2 * spec.quarter
    names = list(inputs) + list(outputs) + ["hi", "lo", "zs"]
    sends = "y" in outputs
    comm = []
    if sends:
        names += ["stage", "sent", "got", "kept"]
        shape = outputs["y"]
        comm = comm_scratch(shape[1:] if kind == "stats" else shape, spec.devs)
    if kind == "enter":
        names += ["psent", "pgot"]
        comm += [pltpu.SemaphoreType.DMA((4,)), pltpu.SemaphoreType.DMA]
    spec.names = names
    vmem = pl.BlockSpec(memory_space=pltpu.VMEM)
    in_specs = [
        pl.BlockSpec(memory_space=pltpu.SMEM) if name in ("code", "freq") else vmem for name in inputs
    ]
    return pl.pallas_call(
        functools.partial(row_kernel, spec),
        out_shape=[jax.ShapeDtypeStruct(shape, f32) for shape in outputs.values()],
        in_specs=in_specs,
        out_specs=[anywhere if name in ("y", "pupil") else vmem for name in outputs],
        scratch_shapes=[
            pltpu.VMEM((4, total, wide), bf16),
            pltpu.VMEM((4, total, wide), bf16),
            pltpu.VMEM((4, total, wide), f32),
        ]
        + comm,
        compiler_params=comm_params(channel) if sends else None,
        name="rows_" + kind,
    )(*inputs.values())


def col_kernel(spec, x_ref, p_ref, w_ref, t_ref, y_ref, hi, lo, zs, stage, sent, got, kept):
    ref = Names(y=y_ref, stage=stage, sent=sent, got=got, kept=kept, same=False)
    me, barrier = greet(spec.devs)
    rows, quarter, devs = spec.rows, spec.quarter, spec.devs
    count_in, count_out, sign = spec.count_in, spec.count_out, spec.sign
    count = p_ref.shape[1]
    per = devs // 4
    weights = (w_ref[0], w_ref[1])
    wide_out = count_out * lanes

    def spread(l):
        at = slice(l * lanes, (l + 1) * lanes)

        def step(i, carry):
            here = pl.ds(pl.multiple_of(i * rows, rows), rows)
            x0, x1, x2, x3 = [x_ref[per * a + i, l] for a in range(4)]
            s, t, d, e = x0 + x2, x1 + x3, x0 - x2, turn(x1 - x3)
            for j, value in enumerate((s + t, d + e, s - t, d - e)):
                if j:
                    value = value * t_ref[0, j - 1, here, :] + turn(value) * t_ref[1, j - 1, here, :]
                high, low = split(value)
                hi[j, here, at] = high
                lo[j, here, at] = low
            return carry

        lax.fori_loop(0, per, step, 0)

    def spectra(first, number):
        span = slice(first * lanes, (first + number) * lanes)
        found = []
        for j in range(4):
            y = dot3(weights, (hi[j, :, span], lo[j, :, span]))
            found.append([])
            for l in range(number):
                at = slice(l * lanes, (l + 1) * lanes)
                found[j].append(y[:quarter, at] + turn(y[quarter:, at]))
        return found

    def pass_on(l, fields):
        at = slice(l * lanes, (l + 1) * lanes)
        for j in range(4):
            high, low = split(fields[j])
            hi[j, :, at] = high
            lo[j, :, at] = low
        for j in range(4):
            y = dot3(weights, (hi[j, :, at], lo[j, :, at]))
            value = y[:quarter] - turn(y[quarter:])
            if j:
                value = value * t_ref[0, j - 1] - turn(value) * t_ref[1, j - 1]
            zs[j, :, at] = value
        if l == 0:
            pl.semaphore_wait(barrier, devs - 1)

        def gather(step, carry):
            i = lax.rem(me + step, per)
            here = pl.ds(pl.multiple_of(i * rows, rows), rows)
            g0, g1, g2, g3 = [zs[j, here, at] for j in range(4)]
            s, t, d, e = g0 + g2, g1 + g3, g0 - g2, turn(g1 - g3)
            for a, value in enumerate((s + t, d - e, s - t, d + e)):
                stage[per * a + i, l] = value
            return carry

        lax.fori_loop(0, per, gather, 0)
        send_all(ref, me, devs, l)

    def shaped(z, l, j):
        return z * p_ref[0, l, j] - sign * (turn(z) * p_ref[1, l, j])

    if count_in == count_out:
        for l in range(count):
            spread(l)
            z = spectra(l, 1)
            pass_on(l, [shaped(z[j][0], l, j) for j in range(4)])
    else:
        for l in range(count_in):
            spread(l)
        z = spectra(0, count_in)
        if count_out == 1:
            pass_on(0, [sum(shaped(z[j][l], l, j) for l in range(count)) for j in range(4)])
        else:
            for j in range(4):
                zs[j, :, wide_out:] = z[j][0]
            for l in range(count):
                pass_on(l, [shaped(zs[j, :, wide_out:], l, j) for j in range(4)])
    finish(ref, me, devs, tuple(range(count_out)))


def run_cols(channel, x, prop, tables, dims, count_in, count_out, sign):
    spec = Names(**vars(dims), count_in=count_in, count_out=count_out, sign=sign)
    rows, quarter, devs = dims.rows, dims.quarter, dims.devs
    wide = max(count_in, count_out) * lanes
    vmem = pl.BlockSpec(memory_space=pltpu.VMEM)
    return pl.pallas_call(
        functools.partial(col_kernel, spec),
        out_shape=jax.ShapeDtypeStruct((devs, count_out, rows, lanes), f32),
        in_specs=[vmem] * 4,
        out_specs=anywhere,
        scratch_shapes=[
            pltpu.VMEM((4, quarter, wide), bf16),
            pltpu.VMEM((4, quarter, wide), bf16),
            pltpu.VMEM((4, quarter, wide + lanes), f32),
        ]
        + comm_scratch((devs, count_out, rows, lanes), devs, count_out),
        compiler_params=comm_params(channel),
        name="cols",
    )(x, prop, jnp.asarray(tables.both), jnp.asarray(tables.twiddle))


def band_kernel(spec, x_ref, p_ref, w_ref, v_ref, y_ref, stage, sent, got, kept):
    ref = Names(y=y_ref, stage=stage, sent=sent, got=got, kept=kept, same=False)
    me, barrier = greet(spec.devs)
    devs, sign, count = spec.devs, spec.sign, spec.count
    half = lanes // 2
    lane = lax.broadcasted_iota(jnp.int32, x_ref.shape[1:], 1)
    pieces = [[], []]
    for s in range(0, devs, 2):
        even, odd = x_ref[s], x_ref[s + 1]
        pieces[0].append(jnp.where(lane < half, even, pltpu.roll(odd, half, 1)))
        pieces[1].append(jnp.where(lane < half, pltpu.roll(even, half, 1), odd))
    field = jnp.concatenate([jnp.concatenate(p, 1) for p in pieces], 0)
    wide = w_ref.shape[2] // 2
    deep = v_ref.shape[2] // 2
    cols = x_ref.shape[1] // 2
    both = dot3(split(field), (w_ref[0], w_ref[1]))
    scaled = []
    for l in range(count):
        re = slice(2 * l * cols, (2 * l + 1) * cols)
        im = slice((2 * l + 1) * cols, (2 * l + 2) * cols)
        yr = both[re, :wide] + both[im, wide:]
        yi = both[im, :wide] - both[re, wide:]
        pr, pi = p_ref[0], sign * p_ref[1]
        scaled += [yr * pr - yi * pi, yr * pi + yi * pr]
    both = dot3(split(jnp.concatenate(scaled, 0)), (v_ref[0], v_ref[1]))
    out = []
    for l in range(count):
        re = slice(2 * l * cols, (2 * l + 1) * cols)
        im = slice((2 * l + 1) * cols, (2 * l + 2) * cols)
        out.append(
            jnp.concatenate(
                [both[re, :deep] - both[im, deep:], both[im, :deep] + both[re, deep:]], 0
            )
        )
    for s in range(0, devs, 2):
        at = slice(s * half, s * half + lanes)
        first, second = out[0][:, at], out[1][:, at]
        stage[s] = jnp.where(lane < half, first, pltpu.roll(second, half, 1))
        stage[s + 1] = jnp.where(lane < half, pltpu.roll(first, half, 1), second)
    pl.semaphore_wait(barrier, devs - 1)
    send_all(ref, me, devs)
    finish(ref, me, devs)


def run_band(channel, x, pupil, tables, dims, sign):
    vmem = pl.BlockSpec(memory_space=pltpu.VMEM)
    return pl.pallas_call(
        functools.partial(band_kernel, Names(**vars(dims), sign=sign)),
        out_shape=jax.ShapeDtypeStruct(x.shape, f32),
        in_specs=[vmem] * 4,
        out_specs=anywhere,
        scratch_shapes=comm_scratch(x.shape, dims.devs),
        compiler_params=comm_params(channel),
        name="pupil_cols",
    )(x, pupil, jnp.asarray(tables.band), jnp.asarray(tables.band_inv))


def body(slab_phase, pupil_phase, pupil_mask, led_code, led_freq, measured):
    devs = lax.axis_size("pat")
    position = lax.axis_index("pat")
    slab_count, rows, size = slab_phase.shape
    patterns, count = led_code.shape
    quarter, cols, per = size // 4, size // devs, devs // 4
    band = 2 * pupil_radius
    band_cols = band // devs
    dims = Names(
        count=count, rows=rows, quarter=quarter, devs=devs, patterns=patterns,
        area=float(size * size),
    )
    rt = row_tables(size, cols, band_cols)
    ct = col_tables(size)
    shape_full = (devs, count, rows, lanes)
    shape_band = (devs, 2 * band_cols, count * rows)
    shape_field = (2, count * rows, size)
    twiddle, table = rt.twiddle, rt

    def near(x):
        return jnp.concatenate([x[:, size - pupil_radius :], x[:, :pupil_radius]], 1)

    opening, phase = near(pupil_mask).astype(f32), near(pupil_phase)
    own = jnp.stack([opening * jnp.cos(phase), opening * jnp.sin(phase)])
    own = jnp.transpose(own.reshape(2, cols // 4, 4, band), (2, 0, 1, 3))
    owners = [(q - pupil_radius // cols) % devs for q in range(per)]

    def wave(freq, index):
        turns = (freq[:, None] * index[None, :]) % size
        angle = turns.astype(f32) * (2.0 * math.pi / size)
        return jnp.stack([jnp.cos(angle), jnp.sin(angle)], 1).reshape(2 * count, -1)

    tilt_c = wave(led_freq[:, 1], jnp.arange(size, dtype=jnp.int32))
    tilt_r = wave(led_freq[:, 0], position * rows + jnp.arange(rows, dtype=jnp.int32))
    tilt_r = jnp.broadcast_to(tilt_r[:, :, None], (2 * count, rows, lanes))
    tilts = dict(tilt_r=tilt_r, tilt_c=tilt_c)
    full_both = dict(inv=table.full_inv, fwd=table.full, twiddle=twiddle)

    one = Names(**{**vars(dims), **dict(count=1)}, leds=count, owners=owners)
    shape_trans = (2, rows, size)
    y, tr0, tr1, tr2, prop, pupil = run_rows(
        7, "enter", None, "full", one,
        dict(slab=slab_phase, own=own, freq=led_freq, fwd=table.full, twiddle=twiddle),
        dict(
            y=(devs, 1, rows, lanes), tr0=shape_trans, tr1=shape_trans, tr2=shape_trans,
            prop=(2, count, 4, quarter, lanes), pupil=(2, band_cols, band),
        ),
    )
    transmission = [tr0, tr1, tr2]
    x = run_cols(1, y, prop, ct, dims, 1, count, 1.0)
    y, passed1 = run_rows(
        8, "forward", "full", "full", dims, dict(x=x, tr=transmission[1], **full_both),
        dict(y=shape_full, passed=shape_field),
    )
    x = run_cols(2, y, prop, ct, dims, count, count, 1.0)
    y, passed2 = run_rows(
        9, "forward_band", "full", "band", dims,
        dict(x=x, tr=transmission[2], inv=table.full_inv, fwd=table.band, twiddle=twiddle, **tilts),
        dict(y=shape_band, passed=shape_field),
    )
    x = run_band(3, y, pupil, ct, dims, 1.0)
    stat_rows = count + count * (count + 1) // 2 + patterns * count + patterns
    dims.stat_rows = stat_rows
    camera, sums = run_rows(
        10, "stats", "band", None, dims,
        dict(x=x, inv=table.band_inv, twiddle=twiddle, measured=measured),
        dict(passed=shape_field, y=(devs, -(-stat_rows // 8) * 8, lanes)),
    )
    (y,) = run_rows(
        11, "weigh", None, "band", dims,
        dict(stats=sums, code=led_code, passed=camera, measured=measured, fwd=table.band, twiddle=twiddle),
        dict(y=shape_band),
    )
    x = run_band(4, y, pupil, ct, dims, -1.0)
    y, grad2 = run_rows(
        12, "back_band", "band", "full", dims,
        dict(x=x, tr=transmission[2], passed=passed2, inv=table.band_inv, fwd=table.full, twiddle=twiddle, **tilts),
        dict(y=shape_full, grad=(rows, size)),
    )
    x = run_cols(5, y, prop, ct, dims, count, count, -1.0)
    y, grad1 = run_rows(
        13, "back", "full", "full", dims,
        dict(x=x, tr=transmission[1], passed=passed1, **full_both),
        dict(y=shape_full, grad=(rows, size)),
    )
    x = run_cols(6, y, prop, ct, dims, count, 1, -1.0)
    (grad0,) = run_rows(
        14, "leave", "full", None, one,
        dict(x=x, tr=transmission[0], inv=table.full_inv, twiddle=twiddle),
        dict(grad=(rows, size)),
    )
    return jnp.stack([grad0, grad1, grad2])


def solution(mesh):
    in_specs = (
        P("tiles", "pat", None),
        P("pat", None),
        P("pat", None),
        P(),
        P(),
        P("tiles", "pat", None),
    )
    out_specs = P("tiles", "pat", None)
    def run(slab_phase, *others):
        devs = mesh.shape["pat"]
        size, count = slab_phase.shape[-1], others[2].shape[1]
        fits = 2 * size == lanes * devs and count * size == lanes * devs and slab_phase.shape[0] == 3 * mesh.shape["tiles"]
        inner = body if fits else plain_body
        return jax.shard_map(inner, mesh=mesh, in_specs=in_specs, out_specs=out_specs, check_vma=False)(
            slab_phase, *others
        )

    return run
```

profile of v0, /device:TPU:4, one launch (start us, length us, event | category | flops | bytes accessed | tf_op | source)
XLA Modules:
  0.0 294.0 jit_solution(5029633020345230293)
XLA Ops:
  0.0 1.0 slice_reduce_fusion
  1.0 0.1 fusion.9
  1.1 1.3 copy.21.refs_1_
  2.5 0.3 fusion.4
  2.8 0.6 reshape.371.refs_6_.refs_7_
  3.5 0.8 fusion.11
  4.3 0.8 fusion.10
  5.1 0.2 cosine_multiply_fusion
  5.3 0.7 maximum_bitcast_fusion.refs_1_
  6.0 0.8 broadcast_in_dim.10.refs_5_.refs_6_
  6.8 20.9 %rows_enter.1 = (f32[16,1,64,128]{3,2,1,0:T(8,128)}, f32[2,64,1024]{2,1,0:T(8,128)}, f32[2,64,1024]{2,1,0:T(8,128)}, f32[2,64,1024]{2,1,0:T(8,128)}, f32[2,2,4,2...) custom-call(f32[3,64,1024]{2,1,0:T(8,128)} %refs_0_.1, f32[4,2,16,256]{3,2,1,0:T(8,128)} %maximum_bitcast_fusion.refs_1_, ...), custom_call_target="tpu_custom_call" | custom-call | tf_op jit(solution)/shard_map/rows_enter/pallas_call | solution.py:686
  27.7 29.3 %cols.4.refs_0_ = f32[16,2,64,128]{3,2,1,0:T(8,128)} custom-call(f32[16,1,64,128]{3,2,1,0:T(8,128)} %get-tuple-element.21.x_ref, f32[2,2,4,256,128]{4,3,2,1,0:T(8,128)} %get-tuple-element.22.p_ref, bf16[2,512,256]{2,1,0:T(8,128)(2,1)} %constant.55.clone.w_ref, f32[2,3,256,128]{3,2,1,0:T(8,128)} %constant.56.clone.t_ref), custom_call_target="tpu_custom_call" | custom-call | tf_op jit(solution)/shard_map/cols/pallas_call | solution.py:794
  57.0 27.0 %rows_forward.1 = (f32[16,2,64,128]{3,2,1,0:T(8,128)}, f32[2,128,1024]{2,1,0:T(8,128)}) custom-call(f32[16,2,64,128]{3,2,1,0:T(8,128)} %cols.4.refs_0_, f32[2,64,1024]{2,1,0:T(8,128)} %get-tuple-element.23.refs_1_, bf16[2,512,512]{2,1,0:T(8,128)(2,1)} %constant.51.clone.refs_2_.refs_3_, bf16[2,512,512]{2,1,0:T(8,128)(2,1)} %constant.50.clone.refs_3_.refs_4_, ...), custom_call_target="tpu_custom_call" | custom-call | tf_op jit(solution)/shard_map/rows_forward/pallas_call | solution.py:686
  84.1 33.0 %cols.5.refs_0_ = f32[16,2,64,128]{3,2,1,0:T(8,128)} custom-call(f32[16,2,64,128]{3,2,1,0:T(8,128)} %get-tuple-element.24.x_ref, f32[2,2,4,256,128]{4,3,2,1,0:T(8,128)} %get-tuple-element.22.p_ref, bf16[2,512,256]{2,1,0:T(8,128)(2,1)} %constant.55.clone.w_ref, f32[2,3,256,128]{3,2,1,0:T(8,128)} %constant.56.clone.t_ref), custom_call_target="tpu_custom_call" | custom-call | tf_op jit(solution)/shard_map/cols/pallas_call | solution.py:794
  117.1 15.2 %rows_forward_band.1 = (f32[16,32,128]{2,1,0:T(8,128)}, f32[2,128,1024]{2,1,0:T(8,128)}) custom-call(f32[16,2,64,128]{3,2,1,0:T(8,128)} %cols.5.refs_0_, f32[2,64,1024]{2,1,0:T(8,128)} %get-tuple-element.25.refs_1_, bf16[2,512,512]{2,1,0:T(8,128)(2,1)} %constant.51.clone.refs_2_.refs_3_, bf16[2,512,128]{2,1,0:T(8,128)(2,1)} %constant.52.clone.refs_3_.refs_4_, ...), custom_call_target="tpu_custom_call" | custom-call | tf_op jit(solution)/shard_map/rows_forward_band/pallas_call | solution.py:686
  132.3 13.0 %pupil_cols.2.refs_0_ = f32[16,32,128]{2,1,0:T(8,128)} custom-call(f32[16,32,128]{2,1,0:T(8,128)} %get-tuple-element.26.x_ref, f32[2,16,256]{2,1,0:T(8,128)} %get-tuple-element.27.p_ref, bf16[2,1024,512]{2,1,0:T(8,128)(2,1)} %constant.57.clone.w_ref, bf16[2,256,2048]{2,1,0:T(8,128)(2,1)} %constant.58.clone.v_ref), custom_call_target="tpu_custom_call" | custom-call | tf_op jit(solution)/shard_map/pupil_cols/pallas_call | solution.py:856
  145.3 11.3 %rows_stats.1 = (f32[2,128,1024]{2,1,0:T(8,128)}, f32[16,24,128]{2,1,0:T(8,128)}) custom-call(f32[16,32,128]{2,1,0:T(8,128)} %pupil_cols.2.refs_0_, bf16[2,128,512]{2,1,0:T(8,128)(2,1)} %constant.53.clone.refs_1_.refs_3_, f32[8,256]{1,0:T(8,128)} %constant.54.clone.refs_4_.refs_2_.refs_5_.refs_3_, s32[4,64,1024]{2,1,0:T(8,128)} %refs_3_.9), custom_call_target="tpu_custom_call" | custom-call | tf_op jit(solution)/shard_map/rows_stats/pallas_call | solution.py:686
  156.7 11.9 %rows_weigh.1.x_ref = f32[16,32,128]{2,1,0:T(8,128)} custom-call(f32[16,24,128]{2,1,0:T(8,128)} %get-tuple-element.28.refs_0_, s32[4,2]{1,0:T(4,128)} %copy.21.refs_1_, f32[2,128,1024]{2,1,0:T(8,128)} %get-tuple-element.29.refs_2_, s32[4,64,1024]{2,1,0:T(8,128)} %refs_3_.9, bf16[2,512,128]{2,1,0:T(8,128)(2,1)} %constant.52.clone.refs_3_.refs_4_, ...), custom_call_target="tpu_custom_call" | custom-call | tf_op jit(solution)/shard_map/rows_weigh/pallas_call | solution.py:686
  168.5 12.6 %pupil_cols.3.refs_0_ = f32[16,32,128]{2,1,0:T(8,128)} custom-call(f32[16,32,128]{2,1,0:T(8,128)} %rows_weigh.1.x_ref, f32[2,16,256]{2,1,0:T(8,128)} %get-tuple-element.27.p_ref, bf16[2,1024,512]{2,1,0:T(8,128)(2,1)} %constant.57.clone.w_ref, bf16[2,256,2048]{2,1,0:T(8,128)(2,1)} %constant.58.clone.v_ref), custom_call_target="tpu_custom_call" | custom-call | tf_op jit(solution)/shard_map/pupil_cols/pallas_call | solution.py:856
  181.1 24.6 %rows_back_band.1 = (f32[16,2,64,128]{3,2,1,0:T(8,128)}, f32[64,1024]{1,0:T(8,128)}) custom-call(f32[16,32,128]{2,1,0:T(8,128)} %pupil_cols.3.refs_0_, f32[2,64,1024]{2,1,0:T(8,128)} %get-tuple-element.25.refs_1_, f32[2,128,1024]{2,1,0:T(8,128)} %get-tuple-element.30.refs_2_, bf16[2,128,512]{2,1,0:T(8,128)(2,1)} %constant.53.clone.refs_1_.refs_3_, ...), custom_call_target="tpu_custom_call" | custom-call | tf_op jit(solution)/shard_map/rows_back_band/pallas_call | solution.py:686
  205.7 33.1 %cols.6.refs_0_ = f32[16,2,64,128]{3,2,1,0:T(8,128)} custom-call(f32[16,2,64,128]{3,2,1,0:T(8,128)} %get-tuple-element.31.x_ref, f32[2,2,4,256,128]{4,3,2,1,0:T(8,128)} %get-tuple-element.22.p_ref, bf16[2,512,256]{2,1,0:T(8,128)(2,1)} %constant.55.clone.w_ref, f32[2,3,256,128]{3,2,1,0:T(8,128)} %constant.56.clone.t_ref), custom_call_target="tpu_custom_call" | custom-call | tf_op jit(solution)/shard_map/cols/pallas_call | solution.py:794
  238.9 26.7 %rows_back.1 = (f32[16,2,64,128]{3,2,1,0:T(8,128)}, f32[64,1024]{1,0:T(8,128)}) custom-call(f32[16,2,64,128]{3,2,1,0:T(8,128)} %cols.6.refs_0_, f32[2,64,1024]{2,1,0:T(8,128)} %get-tuple-element.23.refs_1_, f32[2,128,1024]{2,1,0:T(8,128)} %get-tuple-element.32.refs_2_, bf16[2,512,512]{2,1,0:T(8,128)(2,1)} %constant.51.clone.refs_2_.refs_3_, ...), custom_call_target="tpu_custom_call" | custom-call | tf_op jit(solution)/shard_map/rows_back/pallas_call | solution.py:686
  265.6 22.9 %cols.7.refs_0_ = f32[16,1,64,128]{3,2,1,0:T(8,128)} custom-call(f32[16,2,64,128]{3,2,1,0:T(8,128)} %get-tuple-element.33.x_ref, f32[2,2,4,256,128]{4,3,2,1,0:T(8,128)} %get-tuple-element.22.p_ref, bf16[2,512,256]{2,1,0:T(8,128)(2,1)} %constant.55.clone.w_ref, f32[2,3,256,128]{3,2,1,0:T(8,128)} %constant.56.clone.t_ref), custom_call_target="tpu_custom_call" | custom-call | tf_op jit(solution)/shard_map/cols/pallas_call | solution.py:794
  288.4 0.0 copy-start
  288.4 0.0 copy-start.1
  288.5 3.6 %rows_leave.1 = f32[64,1024]{1,0:T(8,128)} custom-call(f32[16,1,64,128]{3,2,1,0:T(8,128)} %cols.7.refs_0_, f32[2,64,1024]{2,1,0:T(8,128)} %get-tuple-element.34.refs_1_, bf16[2,512,512]{2,1,0:T(8,128)(2,1)} %constant.51.clone.refs_2_.refs_3_, f32[8,256]{1,0:T(8,128)} %constant.54.clone.refs_4_.refs_2_.refs_5_.refs_3_), custom_call_target="tpu_custom_call" | custom-call | tf_op jit(solution)/shard_map/rows_leave/pallas_call | solution.py:686
  292.1 0.0 copy-done
  292.1 0.0 copy-done.1
  292.1 1.9 pad_maximum_fusion
  (7 shorter events, 0.1 us)
Async XLA Ops:
  288.4 3.6 %copy-start = (f32[64,1024]{1,0:T(8,128)S(1)}, f32[64,1024]{1,0:T(8,128)}, u32[]{:S(2)}) copy-start(f32[64,1024]{1,0:T(8,128)} %get-tuple-element.36) | copy-start | bytes 786436
  288.4 3.6 %copy-start.1 = (f32[64,1024]{1,0:T(8,128)S(1)}, f32[64,1024]{1,0:T(8,128)}, u32[]{:S(2)}) copy-start(f32[64,1024]{1,0:T(8,128)} %get-tuple-element.35) | copy-start | bytes 786436
where the time goes:
time: 296 us; the launch traced here: 294 us
  Pallas kernels  285 us (96%)
  local copies, waits for them, and re-layouts  5.3 us (2%)
  other arithmetic  3.3 us (1%)
    pallas_call x8, Pallas kernels, run_rows(): pl.pallas_call(functools.partial(row_kernel, spec), out_shape=[jax.ShapeD...  141 us
    pallas_call x4, Pallas kernels, run_cols(): pl.pallas_call(functools.partial(col_kernel, spec), out_shape=jax.ShapeDt...  118 us
    pallas_call x2, Pallas kernels, run_band(): pl.pallas_call(functools.partial(band_kernel, Names(**vars(dims), sign=si...  25.6 us

commit v1 on v0

v1 whole, which is shorter than its diff:
```python
import functools
import math
import types

import jax
import jax.numpy as jnp
import numpy as np
from jax import lax
from jax.experimental import pallas as pl
from jax.experimental.pallas import tpu as pltpu
from jax.sharding import PartitionSpec as P

spread_rate = 0.3
highest = lax.Precision.HIGHEST


def frequency(grid_index, grid_size):
    return (grid_index + grid_size // 2) % grid_size - grid_size // 2


def complex_times(values, factor):
    real_part = values[0] * factor[0] - values[1] * factor[1]
    imag_part = values[0] * factor[1] + values[1] * factor[0]
    return jnp.stack([real_part, imag_part])


def dft_block(length, direction, norm_factor):
    grid_index = jnp.arange(length, dtype=jnp.int32)
    angles = (grid_index[:, None] * grid_index[None, :] % length).astype(jnp.float32) * (
        2.0 * math.pi / length
    )
    cosine = jnp.cos(angles) * norm_factor
    signed_sine = direction * jnp.sin(angles) * norm_factor
    real_rows = jnp.stack([cosine, signed_sine], 1)
    imag_rows = jnp.stack([-signed_sine, cosine], 1)
    return jnp.stack([real_rows, imag_rows], 0)


def twiddle_table(short_size, long_size, grid_size, direction):
    short_index = jnp.arange(short_size, dtype=jnp.int32)
    long_index = jnp.arange(long_size, dtype=jnp.int32)
    angles = (short_index[:, None] * long_index[None, :] % grid_size).astype(jnp.float32) * (
        2.0 * math.pi / grid_size
    )
    return jnp.stack([jnp.cos(angles), direction * jnp.sin(angles)])


def table_set(col_count, dev_count, grid_size, direction):
    short_table = dft_block(col_count, direction, 1.0)
    long_table = dft_block(dev_count, direction, 1.0 / math.sqrt(grid_size))
    return (short_table, long_table, twiddle_table(col_count, dev_count, grid_size, direction))


def to_fourier(wave_field, tables, dev_count):
    short_table, long_table, twiddles = tables
    led_count = wave_field.shape[1]
    row_count = wave_field.shape[2]
    grid_size = wave_field.shape[3]
    col_count = grid_size // dev_count
    shaped = wave_field.reshape(2, led_count, row_count, col_count, dev_count)
    sectioned = jnp.einsum("zlrmq,zmwc->wlrcq", shaped, short_table, precision=highest)
    sectioned = complex_times(sectioned, twiddles)
    outgoing = jnp.einsum("wlrcq,wqvd->dvlcr", sectioned, long_table, precision=highest)
    incoming = lax.all_to_all(
        outgoing.reshape(dev_count, -1), "pat", split_axis=0, concat_axis=0, tiled=True
    )
    incoming = incoming.reshape(dev_count, 2, led_count, col_count, row_count)
    sectioned = jnp.einsum("swlcr,wsvj->vlcrj", incoming, long_table, precision=highest)
    sectioned = complex_times(sectioned, twiddles)
    sectioned = jnp.einsum("wlcrj,wrvh->vlchj", sectioned, short_table, precision=highest)
    return sectioned.reshape(2, led_count, col_count, grid_size)


def to_space(spectrum, tables, dev_count):
    short_table, long_table, twiddles = tables
    led_count = spectrum.shape[1]
    col_count = spectrum.shape[2]
    grid_size = spectrum.shape[3]
    row_count = grid_size // dev_count
    shaped = spectrum.reshape(2, led_count, col_count, row_count, dev_count)
    sectioned = jnp.einsum("zlcmq,zmwr->wlcrq", shaped, short_table, precision=highest)
    sectioned = complex_times(sectioned, twiddles)
    outgoing = jnp.einsum("wlcrq,wqvd->dvlcr", sectioned, long_table, precision=highest)
    incoming = lax.all_to_all(
        outgoing.reshape(dev_count, -1), "pat", split_axis=0, concat_axis=0, tiled=True
    )
    incoming = incoming.reshape(dev_count, 2, led_count, col_count, row_count)
    sectioned = jnp.einsum("swlcr,wsvj->vlrcj", incoming, long_table, precision=highest)
    sectioned = complex_times(sectioned, twiddles)
    sectioned = jnp.einsum("wlrcj,wcvh->vlrhj", sectioned, short_table, precision=highest)
    return sectioned.reshape(2, led_count, row_count, grid_size)


def plain_body(slab_phase, pupil_phase, pupil_mask, led_code, led_freq, measured):
    dev_count = lax.axis_size("pat")
    position = lax.axis_index("pat")
    slab_count, row_count, grid_size = slab_phase.shape
    col_count = grid_size // dev_count
    pattern_count, led_count = led_code.shape
    area = float(grid_size * grid_size)
    forward_set = table_set(col_count, dev_count, grid_size, -1.0)
    inverse_set = table_set(col_count, dev_count, grid_size, 1.0)
    conjugate = jnp.array([1.0, -1.0], jnp.float32)[:, None, None]
    col_freq = frequency(position * col_count + jnp.arange(col_count, dtype=jnp.int32), grid_size)
    row_freq = frequency(jnp.arange(grid_size, dtype=jnp.int32), grid_size)
    radius = col_freq[:, None] * col_freq[:, None] + row_freq[None, :] * row_freq[None, :]
    cutoff = grid_size // 2 * (grid_size // 2)
    inside = radius <= cutoff
    height = jnp.sqrt(jnp.maximum(cutoff - radius, 0).astype(jnp.float32))
    phase_shift = spread_rate * (height - grid_size // 2)
    propagator = jnp.stack(
        [jnp.where(inside, jnp.cos(phase_shift), 0.0), jnp.where(inside, jnp.sin(phase_shift), 0.0)]
    )
    opening = pupil_mask.astype(jnp.float32)
    pupil = jnp.stack([opening * jnp.cos(pupil_phase), opening * jnp.sin(pupil_phase)])
    propagator_conj = propagator * conjugate
    pupil_conj = pupil * conjugate
    row_index = position * row_count + jnp.arange(row_count, dtype=jnp.int32)
    col_index = jnp.arange(grid_size, dtype=jnp.int32)
    tilt_index = (
        led_freq[:, 0][:, None, None] * row_index[None, :, None]
        + led_freq[:, 1][:, None, None] * col_index[None, None, :]
    ) % grid_size
    tilt_angle = tilt_index.astype(jnp.float32) * (2.0 * math.pi / grid_size)
    illumination = jnp.stack([jnp.cos(tilt_angle), jnp.sin(tilt_angle)])
    transmission = jnp.stack([jnp.cos(slab_phase), jnp.sin(slab_phase)])
    group_count = 1
    group_size = led_count // group_count
    wave_groups = [illumination]
    passed_groups = []
    for slab_index in range(slab_count):
        factor = transmission[:, slab_index]
        passed = [complex_times(wave_field, factor) for wave_field in wave_groups]
        passed_groups.append(passed)
        spectral_factor = propagator if slab_index < slab_count - 1 else pupil
        wave_groups = [
            to_space(
                complex_times(to_fourier(passed_field, forward_set, dev_count), spectral_factor),
                inverse_set,
                dev_count,
            )
            for passed_field in passed
        ]
    camera = wave_groups[0]
    led_power = camera[0] * camera[0] + camera[1] * camera[1]
    code_float = led_code.astype(jnp.float32)
    pattern_power = jnp.dot(
        code_float, led_power.reshape(led_count, -1), precision=highest
    ).reshape(pattern_count, row_count, grid_size)
    counts = measured.astype(jnp.float32)
    power_sum, count_sum = lax.psum(
        (jnp.sum(pattern_power, axis=(1, 2)), jnp.sum(counts, axis=(1, 2))), "pat"
    )
    mean_power = power_sum / area
    mean_count = count_sum / area
    relative = pattern_power / mean_power[:, None, None]
    misfit = relative - counts / mean_count[:, None, None]
    coupling = lax.psum(jnp.sum(misfit * relative, axis=(1, 2)), "pat") / area
    pattern_weight = (misfit - coupling[:, None, None]) / mean_power[:, None, None]
    led_weight = jnp.dot(
        code_float.T, pattern_weight.reshape(pattern_count, -1), precision=highest
    ).reshape(led_count, row_count, grid_size)
    camera_adjoint = 2.0 * led_weight[None] * camera
    adjoint_groups = [camera_adjoint]
    gradients = [None] * slab_count
    for slab_index in range(slab_count - 1, -1, -1):
        spectral_factor = pupil_conj if slab_index == slab_count - 1 else propagator_conj
        back_groups = [
            to_space(
                complex_times(to_fourier(adjoint_field, forward_set, dev_count), spectral_factor),
                inverse_set,
                dev_count,
            )
            for adjoint_field in adjoint_groups
        ]
        gradient = jnp.zeros((row_count, grid_size), jnp.float32)
        for passed_field, back_field in zip(passed_groups[slab_index], back_groups):
            gradient = jnp.sum(
                passed_field[0] * back_field[1] - passed_field[1] * back_field[0], axis=0
            )
        gradients[slab_index] = gradient
        if slab_index > 0:
            release = transmission[:, slab_index] * conjugate
            adjoint_groups = [complex_times(back_field, release) for back_field in back_groups]
    return jnp.stack(gradients)


class Names(types.SimpleNamespace):
    def __getitem__(self, name):
        return getattr(self, name)


pupil_radius = 128
lanes = 128
f32 = jnp.float32
bf16 = jnp.bfloat16


def halves(table):
    table32 = np.asarray(table, np.float32)
    high = table32.astype(bf16)
    low = (table32 - high.astype(np.float32)).astype(bf16)
    return np.stack([high, low])


def row_tables(size, block, band_block):
    quarter = size // 4
    pos = np.arange(quarter)
    angle = 2.0 * np.pi * ((pos[:, None] * pos[None, :]) % quarter) / quarter
    cosine = np.cos(angle) / math.sqrt(size)
    sine = np.sin(angle) / math.sqrt(size)

    def forward(freqs, width):
        parts = []
        for first in range(0, len(freqs), width):
            pick = freqs[first : first + width] % quarter
            left = np.concatenate([cosine[:, pick], sine[:, pick]], 0)
            right = np.concatenate([-sine[:, pick], cosine[:, pick]], 0)
            parts.append(np.concatenate([left, right], 1))
        return np.concatenate(parts, 1)

    full = forward(pos, block)
    reach = pupil_radius // 4
    band = forward(np.arange(-reach, reach), band_block)
    theta = 2.0 * np.pi * (np.arange(4)[:, None] * pos[None, :]) / size
    twiddle = np.concatenate([np.cos(theta), np.sin(theta)], 0).astype(np.float32)
    return Names(
        full=jnp.asarray(halves(full)),
        full_inv=jnp.asarray(halves(full.T)),
        band=jnp.asarray(halves(band)),
        band_inv=jnp.asarray(halves(band.T)),
        twiddle=jnp.asarray(twiddle),
    )


def col_tables(size):
    quarter = size // 4
    pos = np.arange(quarter)
    angle = 2.0 * np.pi * ((pos[:, None] * pos[None, :]) % quarter) / quarter
    both = np.concatenate([np.cos(angle), np.sin(angle)], 0) / math.sqrt(size)
    theta = 2.0 * np.pi * (np.arange(1, 4)[:, None] * pos[None, :]) / size
    twiddle = np.stack([np.cos(theta), np.sin(theta)]).astype(np.float32)
    twiddle = np.ascontiguousarray(np.broadcast_to(twiddle[..., None], twiddle.shape + (lanes,)))
    freqs = np.arange(-pupil_radius, pupil_radius)
    angle = 2.0 * np.pi * ((np.arange(size)[:, None] * freqs[None, :]) % size) / size
    cosine = np.cos(angle) / math.sqrt(size)
    sine = np.sin(angle) / math.sqrt(size)
    band = halves(np.concatenate([cosine, sine], 1))
    band_inv = halves(np.concatenate([cosine.T, sine.T], 1))
    return Names(both=halves(both), twiddle=twiddle, band=band, band_inv=band_inv)


def split(value):
    high = value.astype(bf16)
    return high, (value - high.astype(f32)).astype(bf16)


def dot3(left, right):
    def dot(a, b):
        return jnp.dot(a, b, preferred_element_type=f32)

    return dot(left[0], right[0]) + (dot(left[0], right[1]) + dot(left[1], right[0]))


def turn(value):
    rolled = pltpu.roll(value, lanes // 2, 1)
    lane = lax.broadcasted_iota(jnp.int32, value.shape, 1)
    return jnp.where(lane < lanes // 2, rolled, -rolled)


def row_spread(blocks, twiddle_ref):
    (r0, i0), (r1, i1), (r2, i2), (r3, i3) = blocks
    sr, si, tr, ti = r0 + r2, i0 + i2, r1 + r3, i1 + i3
    dr, di, er, ei = r0 - r2, i0 - i2, r1 - r3, i1 - i3
    mixed = [(sr + tr, si + ti), (dr + ei, di - er), (sr - tr, si - ti), (dr - ei, di + er)]
    out = [mixed[0]]
    for j in range(1, 4):
        cosine, sine = twiddle_ref[j : j + 1, :], twiddle_ref[4 + j : 5 + j, :]
        re, im = mixed[j]
        out.append((re * cosine + im * sine, im * cosine - re * sine))
    return out


def row_gather(parts, twiddle_ref):
    g = [parts[0]]
    for j in range(1, 4):
        cosine, sine = twiddle_ref[j : j + 1, :], twiddle_ref[4 + j : 5 + j, :]
        re, im = parts[j]
        g.append((re * cosine - im * sine, im * cosine + re * sine))
    (r0, i0), (r1, i1), (r2, i2), (r3, i3) = g
    sr, si, tr, ti = r0 + r2, i0 + i2, r1 + r3, i1 + i3
    dr, di, er, ei = r0 - r2, i0 - i2, r1 - r3, i1 - i3
    return [(sr + tr, si + ti), (dr - ei, di + er), (sr - tr, si - ti), (dr + ei, di - er)]


mesh_ids = pl.DeviceIdType.MESH
far_first = (14, 15, 6, 7, 10, 11, 12, 13, 2, 3, 4, 5, 8, 9, 1)
exit_order = (14, 15, 12, 13, 10, 11, 8, 9, 6, 7, 4, 5, 2, 3, 1, 0)


def flip(index, mask):
    out = index
    for bit in (1, 2, 4, 8):
        if mask & bit:
            out = out + bit - 2 * bit * lax.rem(index // bit, 2)
    return out


def whole_kernel(spec, *refs):
    ref = Names(**dict(zip(spec.names, refs)))
    count, rows, quarter, devs, patterns = spec.count, spec.rows, spec.quarter, spec.devs, spec.patterns
    size, per, half, step = 4 * quarter, devs // 4, devs // 2, 16
    tile, place = lax.axis_index("tiles"), lax.axis_index("pat")
    work = place // half
    me = half * tile + lax.rem(place, half)
    native = tile == work
    other = dict(tiles=1 - tile, pat=lax.rem(place + half, devs))

    def member(index):
        return dict(tiles=index // half, pat=work * half + lax.rem(index, half))

    barrier = pltpu.get_barrier_semaphore()
    everyone = spec.tiles * devs

    def signal(hop, carry):
        target = lax.rem(tile * devs + place + hop, everyone)
        pl.semaphore_signal(
            barrier, inc=1, device_id=dict(tiles=target // devs, pat=lax.rem(target, devs)),
            device_id_type=mesh_ids,
        )
        return carry

    lax.fori_loop(1, everyone, signal, 0)

    def local(source, target, sem):
        return pltpu.make_async_copy(source, target, sem)

    def away(source, target, sent, got, device):
        return pltpu.make_async_remote_copy(
            src_ref=source, dst_ref=target, send_sem=sent, recv_sem=got, device_id=device,
            device_id_type=mesh_ids,
        )

    def fetch(name):
        return local(ref[name + "_hbm"], ref[name], ref.loads.at[spec.loaded.index(name)])

    reach = pupil_radius
    spans = (slice(size - reach, size), slice(0, reach))

    def near(name, k):
        return local(ref[name + "_hbm"].at[:, spans[k]], ref[name].at[k], ref[name + "_sem"].at[k])

    for name in ("phase", "mask"):
        for k in range(2):
            near(name, k).start()
    for name in spec.loaded:
        fetch(name).start()

    def ready(name):
        fetch(name).wait()

    def trade(source, target, sent, got):
        @pl.when(native)
        def _():
            local(source, target, got).start()

        @pl.when(jnp.logical_not(native))
        def _():
            away(source, target, sent, got, other).start()

    def trade_slab(s):
        trade(ref.slab_hbm.at[s], ref.slab.at[s], ref.slab_sent.at[s], ref.slab_got.at[s])

    def trade_count(p):
        trade(ref.measured_hbm.at[p], ref.measured.at[p], ref.count_sent.at[p], ref.count_got.at[p])

    def port(name):
        return Names(
            stage=ref[name + "_stage"], y=ref[name + "_y"], sent=ref[name + "_sent"], got=ref[name + "_got"]
        )

    def push(x, slot):
        for mask in far_first:
            dest = flip(me, mask)
            away(
                x.stage.at[slot, dest], x.y.at[slot, me], x.sent.at[slot], x.got.at[slot], member(dest)
            ).start()
        local(x.stage.at[slot, me], x.y.at[slot, me], x.got.at[slot]).start()

    def land(x, slot):
        local(x.y.at[slot], x.y.at[slot], x.got.at[slot]).wait()

    def drain(x, slots):
        for slot in range(slots):
            part = x.stage.at[slot, pl.ds(0, devs - 1)]
            local(part, part, x.sent.at[slot]).wait()

    hi, lo, zs = ref.hi, ref.lo, ref.zs
    cut = [slice(a * quarter, (a + 1) * quarter) for a in range(4)]

    def spot(l, base):
        return pl.ds(pl.multiple_of(l * rows + base, step), step)

    def each_chunk(chunk, carry=0):
        def at_chunk(i, carry):
            base = pl.multiple_of(i * step, step)
            return chunk(base, pl.ds(base, step), carry)

        return lax.fori_loop(0, rows // step, at_chunk, carry)

    def gathered(l, base):
        at = spot(l, base)
        parts = [(zs[j, at, :quarter], zs[j, at, quarter:]) for j in range(4)]
        return row_gather(parts, ref.row_twiddle)

    def scattered(l, base, blocks):
        at = spot(l, base)
        for j, (re, im) in enumerate(row_spread(blocks, ref.row_twiddle)):
            high, low = split(re)
            hi[j, at, :quarter] = high
            lo[j, at, :quarter] = low
            high, low = split(im)
            hi[j, at, quarter:] = high
            lo[j, at, quarter:] = low

    def led_rows(l):
        return pl.ds(pl.multiple_of(l * rows, rows), rows)

    def inverse_full(y, slot, l):
        for j in range(4):
            for q in range(per):
                high, low = split(y[slot, per * j + q])
                ref.ghi[j * rows : (j + 1) * rows, q * lanes : (q + 1) * lanes] = high
                ref.glo[j * rows : (j + 1) * rows, q * lanes : (q + 1) * lanes] = low
        value = dot3((ref.ghi[...], ref.glo[...]), (ref.full_inv[0], ref.full_inv[1]))
        zs[:, led_rows(l), :] = value.reshape(4, rows, 2 * quarter)

    def emit_full(x, slot, l):
        left = [part[:, led_rows(l), :].reshape(4 * rows, 2 * quarter) for part in (hi, lo)]
        value = dot3(left, (ref.full[0], ref.full[1]))
        for j in range(4):
            for q in range(per):
                x.stage[slot, per * j + q] = value[j * rows : (j + 1) * rows, q * lanes : (q + 1) * lanes]
        push(x, slot)

    total = count * rows

    def inverse_band(x):
        for j in range(4):
            block = x.y[0, per * j : per * (j + 1)].reshape(-1, total)
            zs[j, :, :] = dot3(split(block.T), (ref.band_inv[0], ref.band_inv[1]))

    def emit_band(x):
        for j in range(4):
            value = dot3((hi[j], lo[j]), (ref.band[0], ref.band[1]))
            flipped = value.T
            deep = flipped.shape[0] // per
            for q in range(per):
                x.stage[0, per * j + q] = flipped[q * deep : (q + 1) * deep]
        push(x, 0)

    def tilt(l, here, a, value, sign):
        rc, rs = ref.tilt_r[2 * l, here, :], ref.tilt_r[2 * l + 1, here, :]
        cc, cs = ref.tilt_c[2 * l, :, cut[a]], ref.tilt_c[2 * l + 1, :, cut[a]]
        rc = jnp.concatenate([rc] * (quarter // lanes), 1)
        rs = jnp.concatenate([rs] * (quarter // lanes), 1)
        er = rc * cc - rs * cs
        ei = sign * (rc * cs + rs * cc)
        re, im = value
        return re * er - im * ei, re * ei + im * er

    def spread(x, slot):
        def at_part(i, carry):
            here = pl.ds(pl.multiple_of(i * rows, rows), rows)
            x0, x1, x2, x3 = [x.y[slot, per * a + i] for a in range(4)]
            s, t, d, e = x0 + x2, x1 + x3, x0 - x2, turn(x1 - x3)
            for j, value in enumerate((s + t, d + e, s - t, d - e)):
                if j:
                    value = value * ref.col_twiddle[0, j - 1, here, :] + turn(value) * ref.col_twiddle[1, j - 1, here, :]
                high, low = split(value)
                ref.chi[here, j * lanes : (j + 1) * lanes] = high
                ref.clo[here, j * lanes : (j + 1) * lanes] = low
            return carry

        lax.fori_loop(0, per, at_part, 0)

    def col_dot(high, low, take, sign):
        for pair in range(2):
            at = slice(2 * pair * lanes, 2 * (pair + 1) * lanes)
            y = dot3((ref.both[0], ref.both[1]), (high[:, at], low[:, at]))
            for k in range(2):
                at = slice(k * lanes, (k + 1) * lanes)
                take(2 * pair + k, y[:quarter, at] + sign * turn(y[quarter:, at]))

    def shaped(z, l, j, sign):
        return z * ref.prop[0, l, j] - sign * (turn(z) * ref.prop[1, l, j])

    def stow(j, value):
        high, low = split(value)
        ref.dhi[:, j * lanes : (j + 1) * lanes] = high
        ref.dlo[:, j * lanes : (j + 1) * lanes] = low

    def col_inverse(x, slot):
        def take(j, value):
            if j:
                value = value * ref.col_twiddle[0, j - 1] - turn(value) * ref.col_twiddle[1, j - 1]
            ref.cz[j] = value

        col_dot(ref.dhi, ref.dlo, take, -1.0)

        def at_part(i, carry):
            here = pl.ds(pl.multiple_of(i * rows, rows), rows)
            g0, g1, g2, g3 = [ref.cz[j, here, :] for j in range(4)]
            s, t, d, e = g0 + g2, g1 + g3, g0 - g2, turn(g1 - g3)
            for a, value in enumerate((s + t, d - e, s - t, d + e)):
                x.stage[slot, per * a + i] = value
            return carry

        lax.fori_loop(0, per, at_part, 0)

    def each_led(stage):
        def at_led(l, carry):
            stage(l)
            return carry

        lax.fori_loop(0, count, at_led, 0)

    def columns(x, out, sign):
        def stage(l):
            land(x, l)
            spread(x, l)
            col_dot(ref.chi, ref.clo, lambda j, z: stow(j, shaped(z, l, j, sign)), 1.0)
            col_inverse(out, l)
            push(out, l)

        each_led(stage)

    def pupil_columns(x, out, sign):
        land(x, 0)
        middle = lanes // 2
        lane = lax.broadcasted_iota(jnp.int32, x.y.shape[2:], 1)
        pieces = [[], []]
        for s in range(0, devs, 2):
            even, odd = x.y[0, s], x.y[0, s + 1]
            pieces[0].append(jnp.where(lane < middle, even, pltpu.roll(odd, middle, 1)))
            pieces[1].append(jnp.where(lane < middle, pltpu.roll(even, middle, 1), odd))
        field = jnp.concatenate([jnp.concatenate(p, 1) for p in pieces], 0)
        wide = ref.pupil_in.shape[2] // 2
        deep = ref.pupil_out.shape[2] // 2
        cols = x.y.shape[2] // 2
        both = dot3(split(field), (ref.pupil_in[0], ref.pupil_in[1]))
        scaled = []
        for l in range(count):
            re = slice(2 * l * cols, (2 * l + 1) * cols)
            im = slice((2 * l + 1) * cols, (2 * l + 2) * cols)
            yr = both[re, :wide] + both[im, wide:]
            yi = both[im, :wide] - both[re, wide:]
            pr, pi = ref.pupil[0], sign * ref.pupil[1]
            scaled += [yr * pr - yi * pi, yr * pi + yi * pr]
        both = dot3(split(jnp.concatenate(scaled, 0)), (ref.pupil_out[0], ref.pupil_out[1]))
        found = []
        for l in range(count):
            re = slice(2 * l * cols, (2 * l + 1) * cols)
            im = slice((2 * l + 1) * cols, (2 * l + 2) * cols)
            found.append(
                jnp.concatenate(
                    [both[re, :deep] - both[im, deep:], both[im, :deep] + both[re, deep:]], 0
                )
            )
        for s in range(0, devs, 2):
            at = slice(s * middle, s * middle + lanes)
            first, second = found[0][:, at], found[1][:, at]
            out.stage[0, s] = jnp.where(lane < middle, first, pltpu.roll(second, middle, 1))
            out.stage[0, s + 1] = jnp.where(lane < middle, pltpu.roll(first, middle, 1), second)
        push(out, 0)

    def phases(source, target):
        def chunk(base, here, carry):
            phase = source[here, :]
            target[0, here, :] = jnp.cos(phase)
            target[1, here, :] = jnp.sin(phase)
            return carry

        each_chunk(chunk)

    def slab_phases(s):
        local(ref.slab.at[s], ref.slab.at[s], ref.slab_got.at[s]).wait()
        phases(ref.slab.at[s], ref.tr.at[s])

    for name in ("phase", "mask"):
        for k in range(2):
            near(name, k).wait()
    for j in range(4):
        line = pl.ds(j, rows // 4, stride=4)
        for k in range(2):
            opening = ref.mask[k, line, :].astype(f32)
            angle = ref.phase[k, line, :]
            at = slice(k * reach, (k + 1) * reach)
            ref.own[j, 0, :, at] = opening * jnp.cos(angle)
            ref.own[j, 1, :, at] = opening * jnp.sin(angle)
    turn_size = 2.0 * math.pi / size
    col = lax.broadcasted_iota(jnp.int32, (8, size), 1)
    row = me * rows + lax.broadcasted_iota(jnp.int32, (rows, lanes), 0)
    for l in range(count):
        for index, freq, tilts in ((col, ref.freq[l, 1], ref.tilt_c), (row, ref.freq[l, 0], ref.tilt_r)):
            angle = jnp.bitwise_and(index * freq, size - 1).astype(f32) * turn_size
            deep = tilts.shape[1]
            tilts[2 * l] = jnp.cos(angle)[:deep]
            tilts[2 * l + 1] = jnp.sin(angle)[:deep]

    pl.semaphore_wait(barrier, everyone - 1)
    trade_slab(0)

    owners = spec.owners

    def pupil_copy(jj, w, q):
        return away(
            ref.own.at[2 * tile + jj], ref.pupil, ref.pupil_sent.at[2 * jj + w], ref.pupil_got,
            dict(tiles=tile, pat=w * half + jj * per + q),
        )

    for q in range(per):

        @pl.when(place == owners[q])
        def _():
            for jj in range(2):
                for w in range(2):
                    pupil_copy(jj, w, q).start()

    cutoff = size // 2 * (size // 2)

    def centred(index):
        return jnp.where(index >= size // 2, index - size, index)

    def spectrum(i, carry):
        here = pl.ds(pl.multiple_of(i * step, step), step)
        row = lax.broadcasted_iota(jnp.int32, (step, lanes), 0) + i * step
        lane = lax.broadcasted_iota(jnp.int32, (step, lanes), 1)
        lane = jnp.where(lane < lanes // 2, lane, lane - lanes // 2)
        col = 4 * (lax.rem(me, per) * (lanes // 2) + lane) + me // per
        for l in range(count):
            v = centred(col + ref.freq[l, 1])
            for j in range(4):
                u = centred(4 * row + j + ref.freq[l, 0])
                radius = u * u + v * v
                inside = radius <= cutoff
                height = jnp.sqrt(jnp.maximum(cutoff - radius, 0).astype(f32))
                shift = spread_rate * (height - float(size // 2))
                ref.prop[0, l, j, here, :] = jnp.where(inside, jnp.cos(shift), 0.0)
                ref.prop[1, l, j, here, :] = jnp.where(inside, jnp.sin(shift), 0.0)
        return carry

    lax.fori_loop(0, quarter // step, spectrum, 0)

    ready("row_twiddle")
    ready("full")
    local(ref.slab.at[0], ref.slab.at[0], ref.slab_got.at[0]).wait()

    def enter(base, here, carry):
        blocks = []
        for c in cut:
            phase = ref.slab[0, here, c]
            blocks.append((jnp.cos(phase), jnp.sin(phase)))
        scattered(0, base, blocks)
        return carry

    each_chunk(enter)
    x0, x1, x2, x3 = port("x0"), port("x1"), port("x2"), port("x3")
    emit_full(x0, 0, 0)
    trade_slab(1)
    ready("col_twiddle")
    ready("both")
    ready("full_inv")
    land(x0, 0)
    spread(x0, 0)

    def keep_spectrum(j, z):
        ref.cs[j] = z

    col_dot(ref.chi, ref.clo, keep_spectrum, 1.0)

    def first(l):
        for j in range(4):
            stow(j, shaped(ref.cs[j], l, j, 1.0))
        col_inverse(x1, l)
        push(x1, l)

    each_led(first)
    trade_slab(2)
    slab_phases(1)

    def forward(l):
        land(x1, l)
        inverse_full(x1.y, l, l)

        def chunk(base, here, carry):
            fields, at, blocks = gathered(l, base), spot(l, base), []
            for a, c in enumerate(cut):
                tr, ti = ref.tr[1, 0, here, c], ref.tr[1, 1, here, c]
                re, im = fields[a]
                re, im = re * tr - im * ti, re * ti + im * tr
                ref.passed1[0, at, c] = re
                ref.passed1[1, at, c] = im
                blocks.append((re, im))
            scattered(l, base, blocks)
            return carry

        each_chunk(chunk)
        emit_full(x2, l, l)

    each_led(forward)
    for p in range(patterns // 2):
        trade_count(p)
    columns(x2, x3, 1.0)
    for p in range(patterns // 2, patterns):
        trade_count(p)
    slab_phases(2)

    def forward_band(l):
        land(x3, l)
        inverse_full(x3.y, l, l)

        def chunk(base, here, carry):
            fields, at, blocks = gathered(l, base), spot(l, base), []
            for a, c in enumerate(cut):
                tr, ti = ref.tr[2, 0, here, c], ref.tr[2, 1, here, c]
                re, im = fields[a]
                re, im = re * tr - im * ti, re * ti + im * tr
                ref.passed2[0, at, c] = re
                ref.passed2[1, at, c] = im
                blocks.append(tilt(l, here, a, (re, im), 1.0))
            scattered(l, base, blocks)
            return carry

        each_chunk(chunk)

    each_led(forward_band)
    b0, b1, b2, b3, sums = port("b0"), port("b1"), port("b2"), port("b3"), port("sums")
    ready("band")
    emit_band(b0)
    ready("pupil_in")
    ready("pupil_out")
    local(ref.pupil, ref.pupil, ref.pupil_got).wait()
    pupil_columns(b0, b1, 1.0)
    for p in range(patterns):
        local(ref.measured.at[p], ref.measured.at[p], ref.count_got.at[p]).wait()
    ready("band_inv")
    land(b1, 0)
    inverse_band(b1)

    def fold(value):
        total_rows = value[:8]
        for k in range(1, value.shape[0] // 8):
            total_rows = total_rows + value[8 * k : 8 * k + 8]
        out = total_rows[:, :lanes]
        for k in range(1, value.shape[1] // lanes):
            out = out + total_rows[:, lanes * k : lanes * (k + 1)]
        return out

    def measure(base, here, carry):
        fields = [gathered(l, base) for l in range(count)]
        adds = [0.0] * spec.stat_rows
        for a, c in enumerate(cut):
            power = []
            for l in range(count):
                at = spot(l, base)
                re, im = fields[l][a]
                ref.camera[0, at, c] = re
                ref.camera[1, at, c] = im
                power.append(re * re + im * im)
            values = list(power)
            for l in range(count):
                for m in range(l, count):
                    values.append(power[l] * power[m])
            seen = [ref.measured[p, here, c].astype(f32) for p in range(patterns)]
            for p in range(patterns):
                for l in range(count):
                    values.append(seen[p] * power[l])
            values += seen
            for k, value in enumerate(values):
                adds[k] = adds[k] + fold(value)
        return tuple(x + y for x, y in zip(carry, adds))

    stats = each_chunk(measure, tuple(jnp.zeros((8, lanes), f32) for _ in range(spec.stat_rows)))
    packed = [jnp.sum(line, 0, keepdims=True) for line in stats]
    packed.append(jnp.zeros((sums.stage.shape[2] - len(packed), lanes), f32))
    packed = jnp.concatenate(packed, 0)
    for d in range(devs):
        sums.stage[0, d] = packed
    push(sums, 0)
    land(sums, 0)
    added = jnp.sum(jnp.sum(sums.y[0], 0), 1, keepdims=True)
    code = [[ref.code[p, l].astype(f32) for l in range(count)] for p in range(patterns)]
    area = spec.area
    power_mean, count_mean, couple = [], [], []
    base_row = count + count * (count + 1) // 2
    for p in range(patterns):
        mean = sum(added[l : l + 1] * code[p][l] for l in range(count)) / area
        mean_count = added[base_row + patterns * count + p :][:1] / area
        square = 0.0
        at = count
        for l in range(count):
            for m in range(l, count):
                factor = 1.0 if l == m else 2.0
                square = square + (factor * code[p][l] * code[p][m]) * added[at : at + 1]
                at += 1
        cross = sum(code[p][l] * added[base_row + p * count + l :][:1] for l in range(count))
        power_mean.append(mean)
        count_mean.append(mean_count)
        couple.append((square / mean / mean - cross / mean_count / mean) / area)

    def weigh(base, here, carry):
        outgoing = [[] for _ in range(count)]
        for a, c in enumerate(cut):
            camera, power = [], []
            for l in range(count):
                at = spot(l, base)
                re, im = ref.camera[0, at, c], ref.camera[1, at, c]
                camera.append((re, im))
                power.append(re * re + im * im)
            weight = [0.0] * count
            for p in range(patterns):
                lit = sum(code[p][l] * power[l] for l in range(count))
                seen = ref.measured[p, here, c].astype(f32)
                misfit = lit * (1.0 / power_mean[p]) - seen * (1.0 / count_mean[p])
                pull = (misfit - couple[p]) * (1.0 / power_mean[p])
                for l in range(count):
                    weight[l] = weight[l] + code[p][l] * pull
            for l in range(count):
                scale = 2.0 * weight[l]
                outgoing[l].append((scale * camera[l][0], scale * camera[l][1]))
        for l in range(count):
            scattered(l, base, outgoing[l])
        return carry

    each_chunk(weigh)
    emit_band(b2)
    pupil_columns(b2, b3, -1.0)
    land(b3, 0)
    inverse_band(b3)
    y2, y1, y0, out = port("y2"), port("y1"), port("y0"), port("out")
    y3 = port("y3")
    ref.grad[...] = jnp.zeros(ref.grad.shape, f32)

    def back_band(l):
        def chunk(base, here, carry):
            fields, at, blocks = gathered(l, base), spot(l, base), []
            for a, c in enumerate(cut):
                re, im = tilt(l, here, a, fields[a], -1.0)
                pr, pi = ref.passed2[0, at, c], ref.passed2[1, at, c]
                ref.grad[1, here, c] += pr * im - pi * re
                tr, ti = ref.tr[2, 0, here, c], ref.tr[2, 1, here, c]
                blocks.append((re * tr + im * ti, im * tr - re * ti))
            scattered(l, base, blocks)
            return carry

        each_chunk(chunk)
        emit_full(y3, l, l)

    each_led(back_band)
    trade(ref.grad.at[1], ref.result.at[2], ref.grad_sent.at[1], ref.grad_got.at[1])
    columns(y3, y2, -1.0)

    def back(l):
        land(y2, l)
        inverse_full(y2.y, l, l)

        def chunk(base, here, carry):
            fields, at, blocks = gathered(l, base), spot(l, base), []
            for a, c in enumerate(cut):
                re, im = fields[a]
                pr, pi = ref.passed1[0, at, c], ref.passed1[1, at, c]
                ref.grad[0, here, c] += pr * im - pi * re
                tr, ti = ref.tr[1, 0, here, c], ref.tr[1, 1, here, c]
                blocks.append((re * tr + im * ti, im * tr - re * ti))
            scattered(l, base, blocks)
            return carry

        each_chunk(chunk)
        emit_full(y1, l, l)

    each_led(back)
    trade(ref.grad.at[0], ref.result.at[1], ref.grad_sent.at[0], ref.grad_got.at[0])
    ready("slab_own")
    phases(ref.slab_own, ref.tr.at[0])
    ref.cs[...] = jnp.zeros(ref.cs.shape, f32)

    def last(l):
        land(y1, l)
        spread(y1, l)

        def add(j, z):
            ref.cs[j] += shaped(z, l, j, -1.0)

        col_dot(ref.chi, ref.clo, add, 1.0)

    each_led(last)
    for j in range(4):
        stow(j, ref.cs[j])
    col_inverse(y0, 0)
    for mask in exit_order:
        dest = flip(place, mask)
        if mask:
            away(
                y0.stage.at[0, dest], y0.y.at[0, me], y0.sent.at[0], y0.got.at[0],
                dict(tiles=work, pat=dest),
            ).start()
        else:

            @pl.when(native)
            def _():
                local(y0.stage.at[0, dest], y0.y.at[0, me], y0.got.at[0]).start()

            @pl.when(jnp.logical_not(native))
            def _():
                away(
                    y0.stage.at[0, dest], y0.y.at[0, me], y0.sent.at[0], y0.got.at[0],
                    dict(tiles=work, pat=dest),
                ).start()

    land(y0, 0)
    inverse_full(y0.y, 0, 0)

    def leave(base, here, carry):
        fields = gathered(0, base)
        for a, c in enumerate(cut):
            tr, ti = ref.tr[0, 0, here, c], ref.tr[0, 1, here, c]
            re, im = fields[a]
            ref.grad0[here, c] = tr * im - ti * re
        return carry

    each_chunk(leave)
    final = local(ref.grad0, ref.result.at[0], ref.loads.at[len(spec.loaded)])
    final.start()

    for x, slots in (
        (x0, 1), (x1, count), (x2, count), (x3, count), (b0, 1), (b1, 1), (b2, 1), (b3, 1),
        (sums, 1), (y3, count), (y2, count), (y1, count), (y0, 1),
    ):
        drain(x, slots)
    for q in range(per):

        @pl.when(place == owners[q])
        def _():
            for jj in range(2):
                for w in range(2):
                    pupil_copy(jj, w, q).wait_send()

    for k in range(2):
        local(ref.grad.at[k], ref.result.at[k + 1], ref.grad_got.at[k]).wait()

    @pl.when(jnp.logical_not(native))
    def _():
        part = y0.stage.at[0, 0]
        local(part, part, y0.sent.at[0]).wait()
        for s in range(3):
            local(ref.slab.at[s], ref.slab.at[s], ref.slab_sent.at[s]).wait()
        for p in range(patterns):
            local(ref.measured.at[p], ref.measured.at[p], ref.count_sent.at[p]).wait()
        for k in range(2):
            local(ref.grad.at[k], ref.grad.at[k], ref.grad_sent.at[k]).wait()

    final.wait()


def body(tiles, slab_phase, pupil_phase, pupil_mask, led_code, led_freq, measured):
    devs = lax.axis_size("pat")
    slab_count, rows, size = slab_phase.shape
    patterns, count = led_code.shape
    quarter, cols, per = size // 4, size // devs, devs // 4
    band = 2 * pupil_radius
    band_cols = band // devs
    rt = row_tables(size, cols, band_cols)
    ct = col_tables(size)
    stat_rows = count + count * (count + 1) // 2 + patterns * count + patterns
    owners = [(q - pupil_radius // cols) % devs for q in range(per)]
    loads = dict(
        row_twiddle=rt.twiddle, full=rt.full,
        col_twiddle=jnp.asarray(ct.twiddle), both=jnp.asarray(ct.both), full_inv=rt.full_inv, band=rt.band,
        pupil_in=jnp.asarray(ct.band), pupil_out=jnp.asarray(ct.band_inv), band_inv=rt.band_inv,
        slab_own=slab_phase[0],
    )
    inputs = {name + "_hbm": value for name, value in loads.items()}
    inputs |= dict(phase_hbm=pupil_phase, mask_hbm=pupil_mask, slab_hbm=slab_phase, measured_hbm=measured, freq=led_freq, code=led_code)
    wide = 2 * quarter
    total = count * rows
    vmem, dma = pltpu.VMEM, pltpu.SemaphoreType.DMA
    scratch = {name: vmem(value.shape, value.dtype) for name, value in loads.items()}
    scratch |= dict(
        slab=vmem(slab_phase.shape, f32), measured=vmem(measured.shape, jnp.int32),
        phase=vmem((2, rows, pupil_radius), f32), mask=vmem((2, rows, pupil_radius), jnp.int32),
        phase_sem=dma((2,)), mask_sem=dma((2,)), own=vmem((4, 2, rows // 4, band), f32), pupil=vmem((2, band_cols, band), f32),
        tilt_c=vmem((2 * count, 1, size), f32), tilt_r=vmem((2 * count, rows, lanes), f32),
        prop=vmem((2, count, 4, quarter, lanes), f32), tr=vmem((3, 2, rows, size), f32),
        passed1=vmem((2, total, size), f32), passed2=vmem((2, total, size), f32),
        camera=vmem((2, total, size), f32), grad=vmem((2, rows, size), f32), grad0=vmem((rows, size), f32),
        hi=vmem((4, total, wide), bf16), lo=vmem((4, total, wide), bf16), zs=vmem((4, total, wide), f32),
        ghi=vmem((4 * rows, wide), bf16), glo=vmem((4 * rows, wide), bf16),
        chi=vmem((quarter, 4 * lanes), bf16), clo=vmem((quarter, 4 * lanes), bf16),
        dhi=vmem((quarter, 4 * lanes), bf16), dlo=vmem((quarter, 4 * lanes), bf16),
        cz=vmem((4, quarter, lanes), f32), cs=vmem((4, quarter, lanes), f32),
        loads=dma((len(loads) + 1,)),
        slab_sent=dma((3,)), slab_got=dma((3,)), count_sent=dma((patterns,)), count_got=dma((patterns,)),
        pupil_sent=dma((4,)), pupil_got=dma, grad_sent=dma((2,)), grad_got=dma((2,)),
    )
    block, narrow = (devs, rows, lanes), (devs, 2 * band_cols, total)
    ports = dict(x0=(1, block), x1=(count, block), x2=(count, block), x3=(count, block))
    ports |= dict(b0=(1, narrow), b1=(1, narrow), b2=(1, narrow), b3=(1, narrow))
    ports |= dict(sums=(1, (devs, -(-stat_rows // 8) * 8, lanes)))
    ports |= dict(y3=(count, block), y2=(count, block), y1=(count, block), y0=(1, block), out=(1, (8, lanes)))
    for name, (slots, shape) in ports.items():
        scratch[name + "_stage"] = vmem((slots,) + shape, f32)
        scratch[name + "_y"] = vmem((slots,) + shape, f32)
        scratch[name + "_sent"] = dma((slots,))
        scratch[name + "_got"] = dma((slots,))
    spec = Names(
        count=count, rows=rows, quarter=quarter, devs=devs, tiles=tiles, patterns=patterns,
        area=float(size * size), stat_rows=stat_rows, owners=owners, loaded=list(loads),
        names=list(inputs) + ["result"] + list(scratch),
    )
    anywhere = pl.BlockSpec(memory_space=pl.ANY)
    smem = pl.BlockSpec(memory_space=pltpu.SMEM)
    return pl.pallas_call(
        functools.partial(whole_kernel, spec),
        out_shape=jax.ShapeDtypeStruct(slab_phase.shape, f32),
        in_specs=[smem if name in ("freq", "code") else anywhere for name in inputs],
        out_specs=anywhere,
        scratch_shapes=list(scratch.values()),
        compiler_params=pltpu.CompilerParams(
            collective_id=1, has_side_effects=True, vmem_limit_bytes=67043328
        ),
        name="whole",
    )(*inputs.values())


def solution(mesh):
    in_specs = (
        P("tiles", "pat", None),
        P("pat", None),
        P("pat", None),
        P(),
        P(),
        P("tiles", "pat", None),
    )
    out_specs = P("tiles", "pat", None)

    def run(slab_phase, *others):
        devs, tiles = mesh.shape["pat"], mesh.shape["tiles"]
        size, count = slab_phase.shape[-1], others[2].shape[1]
        fits = 2 * size == lanes * devs and count * size == lanes * devs and slab_phase.shape[0] == 3 * tiles
        fits = fits and tiles == 2 and devs == len(exit_order)
        inner = functools.partial(body, tiles) if fits else plain_body
        return jax.shard_map(inner, mesh=mesh, in_specs=in_specs, out_specs=out_specs, check_vma=False)(
            slab_phase, *others
        )

    return run
```

time: 296 us -> 212 us (0.72)
  Pallas kernels: 285 us -> 203 us
  other arithmetic: 3.3 us -> 0 us
    pallas_call x14 -> x1, Pallas kernels: 285 us -> 203 us  [body(): pl.pallas_call(functools.partial(whole_kernel, spec), out_shape=jax.Shape...]
where the time goes in v1:
time: 212 us; the launch traced here: 208 us
  Pallas kernels  203 us (96%)
  local copies, waits for them, and re-layouts  5.11 us (2%)
    pallas_call x1, Pallas kernels, body(): pl.pallas_call(functools.partial(whole_kernel, spec), out_shape=jax.Shape...  203 us

profile of v1, /device:TPU:4, one launch (start us, length us, event | category | flops | bytes accessed | tf_op | source)
XLA Modules:
  0.0 207.8 jit_solution(9840849131909936072)
XLA Ops:
  0.0 1.3 copy.16.refs_15_
  1.3 1.7 slice_bitcast_fusion.refs_9_
  3.0 202.7 %whole.1 = f32[3,64,1024]{2,1,0:T(8,128)} custom-call(f32[8,256]{1,0:T(8,128)} %constant.22.clone.refs_0_, bf16[2,512,512]{2,1,0:T(8,128)(2,1)} %constant.18.clone.refs_1_, f32[2,3,256,128]{3,2,1,0:T(8,128)} %constant.23.clone.refs_2_, bf16[2,512,256]{2,1,0:T(8,128)(2,1)} %constant.24.clone.refs_3_, bf16[2,512,512]{2,1,0:T(8,128)(2,1)} %constant.19.clone.refs_4_, ...), custom_call_target="tpu_custom_call" | custom-call | tf_op jit(solution)/shard_map/whole/pallas_call | solution.py:1023
  205.7 2.1 %copy.18 = f32[3,64,1024]{2,1,0:T(8,128)} copy(f32[3,64,1024]{2,1,0:T(8,128)} %whole.1) | data formatting | bytes 1572864

commit v2 on v1

--- a/solution.py
+++ b/solution.py
@@ -294,8 +294,7 @@
 
 
 mesh_ids = pl.DeviceIdType.MESH
-far_first = (14, 15, 6, 7, 10, 11, 12, 13, 2, 3, 4, 5, 8, 9, 1)
-exit_order = (14, 15, 12, 13, 10, 11, 8, 9, 6, 7, 4, 5, 2, 3, 1, 0)
+far_first = (14, 15, 6, 7, 10, 11, 12, 13, 2, 3, 4, 5, 8, 9, 1, 0)
 
 
 def flip(index, mask):
@@ -314,6 +313,7 @@
     work = place // half
     me = half * tile + lax.rem(place, half)
     native = tile == work
+    foreign = jnp.logical_not(native)
     other = dict(tiles=1 - tile, pat=lax.rem(place + half, devs))
 
     def member(index):
@@ -342,7 +342,8 @@
         )
 
     def fetch(name):
-        return local(ref[name + "_hbm"], ref[name], ref.loads.at[spec.loaded.index(name)])
+        source = ref.slab_hbm.at[0] if name == "slab_own" else ref[name + "_hbm"]
+        return local(source, ref[name], ref.loads.at[spec.loaded.index(name)])
 
     reach = pupil_radius
     spans = (slice(size - reach, size), slice(0, reach))
@@ -359,33 +360,115 @@
     def ready(name):
         fetch(name).wait()
 
-    def trade(source, target, sent, got):
+    share = rows // 2
+    neighbour = dict(tiles=1 - tile, pat=place)
+    across = dict(tiles=tile, pat=lax.rem(place + half, devs))
+
+    sources = dict(slab=ref.slab_hbm, lit=ref.lit_own, grad=ref.grad)
+    targets = dict(slab=ref.slab, lit=ref.lit, grad=ref.result.at[1:3])
+    part = dict(slab=3, lit=spec.sets, grad=2)
+
+    def semaphore(name, kind, k):
+        return ref[name + kind].at[k]
+
+    def direct(name, k):
+        return away(
+            sources[name].at[k, :share], targets[name].at[k, :share], semaphore(name, "_sent", k),
+            semaphore(name, "_got", k), other,
+        )
+
+    def hop(name, k):
+        return away(
+            sources[name].at[k, share:], ref[name + "_relay"].at[k], semaphore(name, "_sent", k),
+            semaphore(name, "_via", k), neighbour,
+        )
+
+    def onward(name, k):
+        return away(
+            ref[name + "_relay"].at[k], targets[name].at[k, share:], semaphore(name, "_sent", k),
+            semaphore(name, "_late" if name == "slab" else "_got", k), across,
+        )
+
+    def trade_native(name, k):
         @pl.when(native)
         def _():
-            local(source, target, got).start()
-
-        @pl.when(jnp.logical_not(native))
+            if name == "slab":
+                for span, kind in ((pl.ds(0, share), "_got"), (pl.ds(share, share), "_late")):
+                    local(sources[name].at[k, span], targets[name].at[k, span], semaphore(name, kind, k)).start()
+            else:
+                local(sources[name].at[k], targets[name].at[k], semaphore(name, "_got", k)).start()
+
+    def trade_foreign(name, *blocks):
+        @pl.when(foreign)
         def _():
-            away(source, target, sent, got, other).start()
-
-    def trade_slab(s):
-        trade(ref.slab_hbm.at[s], ref.slab.at[s], ref.slab_sent.at[s], ref.slab_got.at[s])
-
-    def trade_count(p):
-        trade(ref.measured_hbm.at[p], ref.measured.at[p], ref.count_sent.at[p], ref.count_got.at[p])
+            for k in blocks:
+                direct(name, k).start()
+                hop(name, k).start()
+
+    def forward_on(name, *blocks):
+        @pl.when(native)
+        def _():
+            for k in blocks:
+                hop(name, k).wait_recv()
+                onward(name, k).start()
+
+    def traded(name, k):
+        whole = targets[name].at[k]
+        if name == "slab":
+            halves = (whole.at[:share], whole.at[share:])
+            local(halves[0], halves[0], semaphore(name, "_got", k)).wait()
+            local(halves[1], halves[1], semaphore(name, "_late", k)).wait()
+        else:
+            local(whole, whole, semaphore(name, "_got", k)).wait()
+
+    def trade_ends(name):
+        for k in range(part[name]):
+
+            @pl.when(native)
+            def _():
+                onward(name, k).wait_send()
+
+            @pl.when(foreign)
+            def _():
+                whole = sources[name].at[k]
+                local(whole, whole, semaphore(name, "_sent", k)).wait()
 
     def port(name):
         return Names(
             stage=ref[name + "_stage"], y=ref[name + "_y"], sent=ref[name + "_sent"], got=ref[name + "_got"]
         )
 
+    def push_one(x, slot, mask, span=None):
+        dest = flip(me, mask)
+        source = x.stage.at[slot, dest] if span is None else x.stage.at[slot, dest, span]
+        target = x.y.at[slot, me] if span is None else x.y.at[slot, me, span]
+        if mask:
+            away(source, target, x.sent.at[slot], x.got.at[slot], member(dest)).start()
+        else:
+            local(source, target, x.got.at[slot]).start()
+
     def push(x, slot):
         for mask in far_first:
-            dest = flip(me, mask)
+            push_one(x, slot, mask)
+
+    def leave_one(x, slot, mask):
+        dest = flip(place, mask)
+
+        def start_away():
             away(
-                x.stage.at[slot, dest], x.y.at[slot, me], x.sent.at[slot], x.got.at[slot], member(dest)
+                x.stage.at[slot, dest], x.y.at[slot, me], x.sent.at[slot], x.got.at[slot],
+                dict(tiles=work, pat=dest),
             ).start()
-        local(x.stage.at[slot, me], x.y.at[slot, me], x.got.at[slot]).start()
+
+        if mask:
+            start_away()
+        else:
+
+            @pl.when(native)
+            def _():
+                local(x.stage.at[slot, dest], x.y.at[slot, me], x.got.at[slot]).start()
+
+            pl.when(foreign)(start_away)
 
     def land(x, slot):
         local(x.y.at[slot], x.y.at[slot], x.got.at[slot]).wait()
@@ -500,23 +583,23 @@
         ref.dhi[:, j * lanes : (j + 1) * lanes] = high
         ref.dlo[:, j * lanes : (j + 1) * lanes] = low
 
-    def col_inverse(x, slot):
+    def col_inverse(x, slot, send=push_one, far_parts=(3, 1, 2, 0)):
         def take(j, value):
             if j:
                 value = value * ref.col_twiddle[0, j - 1] - turn(value) * ref.col_twiddle[1, j - 1]
             ref.cz[j] = value
 
         col_dot(ref.dhi, ref.dlo, take, -1.0)
-
-        def at_part(i, carry):
+        home = lax.rem(me, per)
+        for bits in (3, 2, 1, 0):
+            i = flip(home, bits)
             here = pl.ds(pl.multiple_of(i * rows, rows), rows)
             g0, g1, g2, g3 = [ref.cz[j, here, :] for j in range(4)]
             s, t, d, e = g0 + g2, g1 + g3, g0 - g2, turn(g1 - g3)
             for a, value in enumerate((s + t, d - e, s - t, d + e)):
                 x.stage[slot, per * a + i] = value
-            return carry
-
-        lax.fori_loop(0, per, at_part, 0)
+            for far in far_parts:
+                send(x, slot, per * far + bits)
 
     def each_led(stage):
         def at_led(l, carry):
@@ -531,7 +614,6 @@
             spread(x, l)
             col_dot(ref.chi, ref.clo, lambda j, z: stow(j, shaped(z, l, j, sign)), 1.0)
             col_inverse(out, l)
-            push(out, l)
 
         each_led(stage)
 
@@ -583,9 +665,71 @@
 
         each_chunk(chunk)
 
+    def fold(value):
+        total_rows = value[:8]
+        for k in range(1, value.shape[0] // 8):
+            total_rows = total_rows + value[8 * k : 8 * k + 8]
+        out = total_rows[:, :lanes]
+        for k in range(1, value.shape[1] // lanes):
+            out = out + total_rows[:, lanes * k : lanes * (k + 1)]
+        return out
+
+    def fold_all(p):
+        def chunk(base, here, carry):
+            return carry + fold(ref.measured[p, here, :].astype(f32))
+
+        return jnp.sum(each_chunk(chunk, jnp.zeros((8, lanes), f32)), 0, keepdims=True)
+
     def slab_phases(s):
-        local(ref.slab.at[s], ref.slab.at[s], ref.slab_got.at[s]).wait()
+        traded("slab", s)
         phases(ref.slab.at[s], ref.tr.at[s])
+
+    for k in range(3):
+        trade_native("slab", k)
+    turn_size = 2.0 * math.pi / size
+    col = lax.broadcasted_iota(jnp.int32, (8, size), 1)
+    row = me * rows + lax.broadcasted_iota(jnp.int32, (rows, lanes), 0)
+    for l in range(count):
+        for index, freq, tilts in ((col, ref.freq[l, 1], ref.tilt_c), (row, ref.freq[l, 0], ref.tilt_r)):
+            angle = jnp.bitwise_and(index * freq, size - 1).astype(f32) * turn_size
+            deep = tilts.shape[1]
+            tilts[2 * l] = jnp.cos(angle)[:deep]
+            tilts[2 * l + 1] = jnp.sin(angle)[:deep]
+
+    pl.semaphore_wait(barrier, everyone - 1)
+    trade_foreign("slab", 0, 1, 2)
+    ready("row_twiddle")
+    ready("full")
+    x0, x1, x2, x3 = port("x0"), port("x1"), port("x2"), port("x3")
+
+    def enter(first, count_rows):
+        def chunk(i, carry):
+            base = pl.multiple_of(first + i * step, step)
+            here = pl.ds(base, step)
+            blocks = []
+            for c in cut:
+                phase = ref.slab[0, here, c]
+                blocks.append((jnp.cos(phase), jnp.sin(phase)))
+            scattered(0, base, blocks)
+            return carry
+
+        lax.fori_loop(0, count_rows // step, chunk, 0)
+        span = pl.ds(first, count_rows)
+        left = [part[:, span, :].reshape(4 * count_rows, 2 * quarter) for part in (hi, lo)]
+        value = dot3(left, (ref.full[0], ref.full[1]))
+        for j in range(4):
+            for q in range(per):
+                x0.stage[0, per * j + q, span] = value[
+                    j * count_rows : (j + 1) * count_rows, q * lanes : (q + 1) * lanes
+                ]
+        for mask in far_first:
+            push_one(x0, 0, mask, span)
+
+    @pl.when(native)
+    def _():
+        traded("slab", 0)
+        enter(0, rows)
+
 
     for name in ("phase", "mask"):
         for k in range(2):
@@ -598,19 +742,6 @@
             at = slice(k * reach, (k + 1) * reach)
             ref.own[j, 0, :, at] = opening * jnp.cos(angle)
             ref.own[j, 1, :, at] = opening * jnp.sin(angle)
-    turn_size = 2.0 * math.pi / size
-    col = lax.broadcasted_iota(jnp.int32, (8, size), 1)
-    row = me * rows + lax.broadcasted_iota(jnp.int32, (rows, lanes), 0)
-    for l in range(count):
-        for index, freq, tilts in ((col, ref.freq[l, 1], ref.tilt_c), (row, ref.freq[l, 0], ref.tilt_r)):
-            angle = jnp.bitwise_and(index * freq, size - 1).astype(f32) * turn_size
-            deep = tilts.shape[1]
-            tilts[2 * l] = jnp.cos(angle)[:deep]
-            tilts[2 * l + 1] = jnp.sin(angle)[:deep]
-
-    pl.semaphore_wait(barrier, everyone - 1)
-    trade_slab(0)
-
     owners = spec.owners
 
     def pupil_copy(jj, w, q):
@@ -627,6 +758,7 @@
                 for w in range(2):
                     pupil_copy(jj, w, q).start()
 
+    forward_on("slab", 0)
     cutoff = size // 2 * (size // 2)
 
     def centred(index):
@@ -650,24 +782,35 @@
                 ref.prop[1, l, j, here, :] = jnp.where(inside, jnp.sin(shift), 0.0)
         return carry
 
-    lax.fori_loop(0, quarter // step, spectrum, 0)
-
-    ready("row_twiddle")
-    ready("full")
-    local(ref.slab.at[0], ref.slab.at[0], ref.slab_got.at[0]).wait()
-
-    def enter(base, here, carry):
-        blocks = []
-        for c in cut:
-            phase = ref.slab[0, here, c]
-            blocks.append((jnp.cos(phase), jnp.sin(phase)))
-        scattered(0, base, blocks)
-        return carry
-
-    each_chunk(enter)
-    x0, x1, x2, x3 = port("x0"), port("x1"), port("x2"), port("x3")
-    emit_full(x0, 0, 0)
-    trade_slab(1)
+    lax.fori_loop(0, quarter // step // 2, spectrum, 0)
+    forward_on("slab", 1)
+    lax.fori_loop(quarter // step // 2, quarter // step, spectrum, 0)
+
+    @pl.when(foreign)
+    def _():
+        direct("slab", 0).wait_recv()
+        enter(0, share)
+        onward("slab", 0).wait_recv()
+        enter(share, rows - share)
+
+
+    ready("measured")
+    counts = port("counts")
+    lines = [fold_all(p) for p in range(patterns)]
+    lines.append(jnp.zeros((counts.stage.shape[2] - patterns, lanes), f32))
+    lines = jnp.concatenate(lines, 0)
+    for d in range(devs):
+        counts.stage[0, d] = lines
+    for mask in far_first:
+        dest = flip(place, mask)
+        if mask:
+            away(
+                counts.stage.at[0, dest], counts.y.at[0, place], counts.sent.at[0], counts.got.at[0],
+                dict(tiles=tile, pat=dest),
+            ).start()
+        else:
+            local(counts.stage.at[0, dest], counts.y.at[0, place], counts.got.at[0]).start()
+    forward_on("slab", 2)
     ready("col_twiddle")
     ready("both")
     ready("full_inv")
@@ -683,10 +826,33 @@
         for j in range(4):
             stow(j, shaped(ref.cs[j], l, j, 1.0))
         col_inverse(x1, l)
-        push(x1, l)
 
     each_led(first)
-    trade_slab(2)
+    land(counts, 0)
+    count_sum = jnp.sum(jnp.sum(counts.y[0], 0), 1, keepdims=True)
+    area = spec.area
+    code = [[ref.code[l, p].astype(f32) for l in range(count)] for p in range(patterns)]
+    lit_sets = [[l for l in range(count) if (c + 1) >> l & 1] for c in range(spec.sets)]
+    member_of = []
+    for leds in lit_sets:
+        member_of.append([])
+        for p in range(patterns):
+            is_in = 1.0
+            for l in range(count):
+                is_in = is_in * (code[p][l] if l in leds else 1.0 - code[p][l])
+            member_of[-1].append(is_in)
+    share_of = [[member_of[c][p] * (area / count_sum[p : p + 1]) for p in range(patterns)] for c in range(spec.sets)]
+
+    def gather_counts(base, here, carry):
+        for c in cut:
+            seen = [ref.measured[p, here, c].astype(f32) for p in range(patterns)]
+            for k in range(spec.sets):
+                ref.lit_own[k, here, c] = sum(share_of[k][p] * seen[p] for p in range(patterns))
+        return carry
+
+    each_chunk(gather_counts)
+    for k in range(spec.sets):
+        trade_native("lit", k)
     slab_phases(1)
 
     def forward(l):
@@ -709,11 +875,10 @@
         emit_full(x2, l, l)
 
     each_led(forward)
-    for p in range(patterns // 2):
-        trade_count(p)
+    trade_foreign("lit", 0)
     columns(x2, x3, 1.0)
-    for p in range(patterns // 2, patterns):
-        trade_count(p)
+    trade_foreign("lit", *range(1, spec.sets))
+    forward_on("lit", 0)
     slab_phases(2)
 
     def forward_band(l):
@@ -735,6 +900,7 @@
         each_chunk(chunk)
 
     each_led(forward_band)
+    forward_on("lit", *range(1, spec.sets))
     b0, b1, b2, b3, sums = port("b0"), port("b1"), port("b2"), port("b3"), port("sums")
     ready("band")
     emit_band(b0)
@@ -742,20 +908,11 @@
     ready("pupil_out")
     local(ref.pupil, ref.pupil, ref.pupil_got).wait()
     pupil_columns(b0, b1, 1.0)
-    for p in range(patterns):
-        local(ref.measured.at[p], ref.measured.at[p], ref.count_got.at[p]).wait()
+    for k in range(spec.sets):
+        traded("lit", k)
     ready("band_inv")
     land(b1, 0)
     inverse_band(b1)
-
-    def fold(value):
-        total_rows = value[:8]
-        for k in range(1, value.shape[0] // 8):
-            total_rows = total_rows + value[8 * k : 8 * k + 8]
-        out = total_rows[:, :lanes]
-        for k in range(1, value.shape[1] // lanes):
-            out = out + total_rows[:, lanes * k : lanes * (k + 1)]
-        return out
 
     def measure(base, here, carry):
         fields = [gathered(l, base) for l in range(count)]
@@ -772,11 +929,9 @@
             for l in range(count):
                 for m in range(l, count):
                     values.append(power[l] * power[m])
-            seen = [ref.measured[p, here, c].astype(f32) for p in range(patterns)]
-            for p in range(patterns):
-                for l in range(count):
-                    values.append(seen[p] * power[l])
-            values += seen
+            for k, leds in enumerate(lit_sets):
+                seen = ref.lit[k, here, c]
+                values += [seen * power[l] for l in leds]
             for k, value in enumerate(values):
                 adds[k] = adds[k] + fold(value)
         return tuple(x + y for x, y in zip(carry, adds))
@@ -790,24 +945,22 @@
     push(sums, 0)
     land(sums, 0)
     added = jnp.sum(jnp.sum(sums.y[0], 0), 1, keepdims=True)
-    code = [[ref.code[p, l].astype(f32) for l in range(count)] for p in range(patterns)]
-    area = spec.area
-    power_mean, count_mean, couple = [], [], []
-    base_row = count + count * (count + 1) // 2
-    for p in range(patterns):
-        mean = sum(added[l : l + 1] * code[p][l] for l in range(count)) / area
-        mean_count = added[base_row + patterns * count + p :][:1] / area
+    pairs = [(l, m) for l in range(count) for m in range(l, count)]
+    cross_row = count + len(pairs)
+    inverse_mean, number, couple = [], [], []
+    for k, leds in enumerate(lit_sets):
+        mean = sum(added[l : l + 1] for l in leds) / area
+        members = sum(member_of[k])
+        inverse = jnp.where(members > 0.0, 1.0 / mean, 0.0)
         square = 0.0
-        at = count
-        for l in range(count):
-            for m in range(l, count):
-                factor = 1.0 if l == m else 2.0
-                square = square + (factor * code[p][l] * code[p][m]) * added[at : at + 1]
-                at += 1
-        cross = sum(code[p][l] * added[base_row + p * count + l :][:1] for l in range(count))
-        power_mean.append(mean)
-        count_mean.append(mean_count)
-        couple.append((square / mean / mean - cross / mean_count / mean) / area)
+        for at, (l, m) in enumerate(pairs):
+            if l in leds and m in leds:
+                square = square + (1.0 if l == m else 2.0) * added[count + at : count + at + 1]
+        cross = sum(added[cross_row + i : cross_row + i + 1] for i in range(len(leds)))
+        cross_row += len(leds)
+        inverse_mean.append(inverse)
+        number.append(members * inverse)
+        couple.append((members * square * inverse * inverse - cross * inverse) / area)
 
     def weigh(base, here, carry):
         outgoing = [[] for _ in range(count)]
@@ -819,13 +972,11 @@
                 camera.append((re, im))
                 power.append(re * re + im * im)
             weight = [0.0] * count
-            for p in range(patterns):
-                lit = sum(code[p][l] * power[l] for l in range(count))
-                seen = ref.measured[p, here, c].astype(f32)
-                misfit = lit * (1.0 / power_mean[p]) - seen * (1.0 / count_mean[p])
-                pull = (misfit - couple[p]) * (1.0 / power_mean[p])
-                for l in range(count):
-                    weight[l] = weight[l] + code[p][l] * pull
+            for k, leds in enumerate(lit_sets):
+                lit = sum(power[l] for l in leds)
+                pull = (lit * number[k] - ref.lit[k, here, c] - couple[k]) * inverse_mean[k]
+                for l in leds:
+                    weight[l] = weight[l] + pull
             for l in range(count):
                 scale = 2.0 * weight[l]
                 outgoing[l].append((scale * camera[l][0], scale * camera[l][1]))
@@ -838,8 +989,7 @@
     pupil_columns(b2, b3, -1.0)
     land(b3, 0)
     inverse_band(b3)
-    y2, y1, y0, out = port("y2"), port("y1"), port("y0"), port("out")
-    y3 = port("y3")
+    y3, y2, y1, y0 = port("y3"), port("y2"), port("y1"), port("y0")
     ref.grad[...] = jnp.zeros(ref.grad.shape, f32)
 
     def back_band(l):
@@ -855,11 +1005,17 @@
             return carry
 
         each_chunk(chunk)
+
+        @pl.when(l == count - 1)
+        def _():
+            trade_native("grad", 1)
+            trade_foreign("grad", 1)
+
         emit_full(y3, l, l)
 
     each_led(back_band)
-    trade(ref.grad.at[1], ref.result.at[2], ref.grad_sent.at[1], ref.grad_got.at[1])
     columns(y3, y2, -1.0)
+    forward_on("grad", 1)
 
     def back(l):
         land(y2, l)
@@ -877,10 +1033,15 @@
             return carry
 
         each_chunk(chunk)
+
+        @pl.when(l == count - 1)
+        def _():
+            trade_native("grad", 0)
+            trade_foreign("grad", 0)
+
         emit_full(y1, l, l)
 
     each_led(back)
-    trade(ref.grad.at[0], ref.result.at[1], ref.grad_sent.at[0], ref.grad_got.at[0])
     ready("slab_own")
     phases(ref.slab_own, ref.tr.at[0])
     ref.cs[...] = jnp.zeros(ref.cs.shape, f32)
@@ -894,30 +1055,12 @@
 
         col_dot(ref.chi, ref.clo, add, 1.0)
 
-    each_led(last)
+    last(0)
+    forward_on("grad", 0)
+    lax.fori_loop(1, count, lambda l, carry: last(l) or carry, 0)
     for j in range(4):
         stow(j, ref.cs[j])
-    col_inverse(y0, 0)
-    for mask in exit_order:
-        dest = flip(place, mask)
-        if mask:
-            away(
-                y0.stage.at[0, dest], y0.y.at[0, me], y0.sent.at[0], y0.got.at[0],
-                dict(tiles=work, pat=dest),
-            ).start()
-        else:
-
-            @pl.when(native)
-            def _():
-                local(y0.stage.at[0, dest], y0.y.at[0, me], y0.got.at[0]).start()
-
-            @pl.when(jnp.logical_not(native))
-            def _():
-                away(
-                    y0.stage.at[0, dest], y0.y.at[0, me], y0.sent.at[0], y0.got.at[0],
-                    dict(tiles=work, pat=dest),
-                ).start()
-
+    col_inverse(y0, 0, leave_one, (3, 2, 1, 0))
     land(y0, 0)
     inverse_full(y0.y, 0, 0)
 
@@ -935,7 +1078,7 @@
 
     for x, slots in (
         (x0, 1), (x1, count), (x2, count), (x3, count), (b0, 1), (b1, 1), (b2, 1), (b3, 1),
-        (sums, 1), (y3, count), (y2, count), (y1, count), (y0, 1),
+        (sums, 1), (counts, 1), (y3, count), (y2, count), (y1, count), (y0, 1),
     ):
         drain(x, slots)
     for q in range(per):
@@ -946,19 +1089,15 @@
                 for w in range(2):
                     pupil_copy(jj, w, q).wait_send()
 
+    for name in part:
+        trade_ends(name)
     for k in range(2):
-        local(ref.grad.at[k], ref.result.at[k + 1], ref.grad_got.at[k]).wait()
-
-    @pl.when(jnp.logical_not(native))
+        traded("grad", k)
+
+    @pl.when(foreign)
     def _():
-        part = y0.stage.at[0, 0]
-        local(part, part, y0.sent.at[0]).wait()
-        for s in range(3):
-            local(ref.slab.at[s], ref.slab.at[s], ref.slab_sent.at[s]).wait()
-        for p in range(patterns):
-            local(ref.measured.at[p], ref.measured.at[p], ref.count_sent.at[p]).wait()
-        for k in range(2):
-            local(ref.grad.at[k], ref.grad.at[k], ref.grad_sent.at[k]).wait()
+        block = y0.stage.at[0, 0]
+        local(block, block, y0.sent.at[0]).wait()
 
     final.wait()
 
@@ -972,22 +1111,24 @@
     band_cols = band // devs
     rt = row_tables(size, cols, band_cols)
     ct = col_tables(size)
-    stat_rows = count + count * (count + 1) // 2 + patterns * count + patterns
+    sets = 2**count - 1
+    stat_rows = count + count * (count + 1) // 2 + count * 2 ** (count - 1)
     owners = [(q - pupil_radius // cols) % devs for q in range(per)]
     loads = dict(
         row_twiddle=rt.twiddle, full=rt.full,
         col_twiddle=jnp.asarray(ct.twiddle), both=jnp.asarray(ct.both), full_inv=rt.full_inv, band=rt.band,
-        pupil_in=jnp.asarray(ct.band), pupil_out=jnp.asarray(ct.band_inv), band_inv=rt.band_inv,
-        slab_own=slab_phase[0],
+        pupil_in=jnp.asarray(ct.band), pupil_out=jnp.asarray(ct.band_inv), band_inv=rt.band_inv, measured=measured,
     )
     inputs = {name + "_hbm": value for name, value in loads.items()}
-    inputs |= dict(phase_hbm=pupil_phase, mask_hbm=pupil_mask, slab_hbm=slab_phase, measured_hbm=measured, freq=led_freq, code=led_code)
+    inputs |= dict(phase_hbm=pupil_phase, mask_hbm=pupil_mask, slab_hbm=slab_phase, freq=led_freq, code=led_code.T)
     wide = 2 * quarter
     total = count * rows
     vmem, dma = pltpu.VMEM, pltpu.SemaphoreType.DMA
     scratch = {name: vmem(value.shape, value.dtype) for name, value in loads.items()}
+    loads["slab_own"] = None
+    scratch["slab_own"] = vmem((rows, size), f32)
     scratch |= dict(
-        slab=vmem(slab_phase.shape, f32), measured=vmem(measured.shape, jnp.int32),
+        slab=vmem(slab_phase.shape, f32), lit=vmem((sets, rows, size), f32), lit_own=vmem((sets, rows, size), f32),
         phase=vmem((2, rows, pupil_radius), f32), mask=vmem((2, rows, pupil_radius), jnp.int32),
         phase_sem=dma((2,)), mask_sem=dma((2,)), own=vmem((4, 2, rows // 4, band), f32), pupil=vmem((2, band_cols, band), f32),
         tilt_c=vmem((2 * count, 1, size), f32), tilt_r=vmem((2 * count, rows, lanes), f32),
@@ -1000,14 +1141,18 @@
         dhi=vmem((quarter, 4 * lanes), bf16), dlo=vmem((quarter, 4 * lanes), bf16),
         cz=vmem((4, quarter, lanes), f32), cs=vmem((4, quarter, lanes), f32),
         loads=dma((len(loads) + 1,)),
-        slab_sent=dma((3,)), slab_got=dma((3,)), count_sent=dma((patterns,)), count_got=dma((patterns,)),
-        pupil_sent=dma((4,)), pupil_got=dma, grad_sent=dma((2,)), grad_got=dma((2,)),
+        pupil_sent=dma((4,)), pupil_got=dma,
     )
+    for name, blocks in (("slab", 3), ("lit", sets), ("grad", 2)):
+        scratch[name + "_relay"] = vmem((blocks, rows // 2, size), f32)
+        for kind in ("_sent", "_got", "_late", "_via"):
+            scratch[name + kind] = dma((blocks,))
     block, narrow = (devs, rows, lanes), (devs, 2 * band_cols, total)
     ports = dict(x0=(1, block), x1=(count, block), x2=(count, block), x3=(count, block))
     ports |= dict(b0=(1, narrow), b1=(1, narrow), b2=(1, narrow), b3=(1, narrow))
     ports |= dict(sums=(1, (devs, -(-stat_rows // 8) * 8, lanes)))
-    ports |= dict(y3=(count, block), y2=(count, block), y1=(count, block), y0=(1, block), out=(1, (8, lanes)))
+    ports |= dict(counts=(1, (devs, -(-patterns // 8) * 8, lanes)))
+    ports |= dict(y3=(count, block), y2=(count, block), y1=(count, block), y0=(1, block))
     for name, (slots, shape) in ports.items():
         scratch[name + "_stage"] = vmem((slots,) + shape, f32)
         scratch[name + "_y"] = vmem((slots,) + shape, f32)
@@ -1015,7 +1160,7 @@
         scratch[name + "_got"] = dma((slots,))
     spec = Names(
         count=count, rows=rows, quarter=quarter, devs=devs, tiles=tiles, patterns=patterns,
-        area=float(size * size), stat_rows=stat_rows, owners=owners, loaded=list(loads),
+        area=float(size * size), stat_rows=stat_rows, sets=sets, owners=owners, loaded=list(loads),
         names=list(inputs) + ["result"] + list(scratch),
     )
     anywhere = pl.BlockSpec(memory_space=pl.ANY)
@@ -1048,7 +1193,7 @@
         devs, tiles = mesh.shape["pat"], mesh.shape["tiles"]
         size, count = slab_phase.shape[-1], others[2].shape[1]
         fits = 2 * size == lanes * devs and count * size == lanes * devs and slab_phase.shape[0] == 3 * tiles
-        fits = fits and tiles == 2 and devs == len(exit_order)
+        fits = fits and tiles == 2 and devs == len(far_first)
         inner = functools.partial(body, tiles) if fits else plain_body
         return jax.shard_map(inner, mesh=mesh, in_specs=in_specs, out_specs=out_specs, check_vma=False)(
             slab_phase, *others

time: 212 us -> 182 us (0.86)
  Pallas kernels: 203 us -> 177 us
  local copies, waits for them, and re-layouts: 5.11 us -> 2.09 us
    pallas_call x1, Pallas kernels: 203 us -> 177 us  [body(): pl.pallas_call(functools.partial(whole_kernel, spec), out_shape=jax.Shape...]
where the time goes in v2:
time: 182 us; the launch traced here: 179 us
  Pallas kernels  177 us (97%)
  local copies, waits for them, and re-layouts  2.09 us (1%)
    pallas_call x1, Pallas kernels, body(): pl.pallas_call(functools.partial(whole_kernel, spec), out_shape=jax.Shape...  177 us

profile of v2, /device:TPU:4, one launch (start us, length us, event | category | flops | bytes accessed | tf_op | source)
XLA Modules:
  0.0 178.9 jit_solution(3514292949850875613)
XLA Ops:
  0.0 176.8 %whole.1 = f32[3,64,1024]{2,1,0:T(8,128)} custom-call(f32[8,256]{1,0:T(8,128)} %constant.22.clone.refs_0_, bf16[2,512,512]{2,1,0:T(8,128)(2,1)} %constant.18.clone.refs_1_, f32[2,3,256,128]{3,2,1,0:T(8,128)} %constant.23.clone.refs_2_, bf16[2,512,256]{2,1,0:T(8,128)(2,1)} %constant.24.clone.refs_3_, bf16[2,512,512]{2,1,0:T(8,128)(2,1)} %constant.19.clone.refs_4_, ...), custom_call_target="tpu_custom_call" | custom-call | tf_op jit(solution)/shard_map/whole/pallas_call | solution.py:1168
  176.9 2.1 %copy.17 = f32[3,64,1024]{2,1,0:T(8,128)} copy(f32[3,64,1024]{2,1,0:T(8,128)} %whole.1) | data formatting | bytes 1572864

commit v3 on v2

--- a/solution.py
+++ b/solution.py
@@ -241,13 +241,7 @@
     theta = 2.0 * np.pi * (np.arange(1, 4)[:, None] * pos[None, :]) / size
     twiddle = np.stack([np.cos(theta), np.sin(theta)]).astype(np.float32)
     twiddle = np.ascontiguousarray(np.broadcast_to(twiddle[..., None], twiddle.shape + (lanes,)))
-    freqs = np.arange(-pupil_radius, pupil_radius)
-    angle = 2.0 * np.pi * ((np.arange(size)[:, None] * freqs[None, :]) % size) / size
-    cosine = np.cos(angle) / math.sqrt(size)
-    sine = np.sin(angle) / math.sqrt(size)
-    band = halves(np.concatenate([cosine, sine], 1))
-    band_inv = halves(np.concatenate([cosine.T, sine.T], 1))
-    return Names(both=halves(both), twiddle=twiddle, band=band, band_inv=band_inv)
+    return Names(both=halves(both), twiddle=twiddle)
 
 
 def split(value):
@@ -526,21 +520,35 @@
                 x.stage[slot, per * j + q] = value[j * rows : (j + 1) * rows, q * lanes : (q + 1) * lanes]
         push(x, slot)
 
-    total = count * rows
-
-    def inverse_band(x):
-        for j in range(4):
-            block = x.y[0, per * j : per * (j + 1)].reshape(-1, total)
-            zs[j, :, :] = dot3(split(block.T), (ref.band_inv[0], ref.band_inv[1]))
-
-    def emit_band(x):
-        for j in range(4):
-            value = dot3((hi[j], lo[j]), (ref.band[0], ref.band[1]))
-            flipped = value.T
-            deep = flipped.shape[0] // per
-            for q in range(per):
-                x.stage[0, per * j + q] = flipped[q * deep : (q + 1) * deep]
-        push(x, 0)
+    def braid(first, second):
+        middle = lanes // 2
+        lane = lax.broadcasted_iota(jnp.int32, first.shape, 1)
+        return (
+            jnp.where(lane < middle, first, pltpu.roll(second, middle, 1)),
+            jnp.where(lane < middle, pltpu.roll(first, middle, 1), second),
+        )
+
+    def inverse_band(x, l):
+        for pair in range(2):
+            turned = x.y[l, 2 * per * pair : 2 * per * (pair + 1)].reshape(lanes, lanes).T
+            for k, block in enumerate(braid(turned[:rows], turned[rows:])):
+                at = slice((2 * pair + k) * rows, (2 * pair + k + 1) * rows)
+                high, low = split(block)
+                ref.ghi[at, :lanes] = high
+                ref.glo[at, :lanes] = low
+        value = dot3((ref.ghi[:, :lanes], ref.glo[:, :lanes]), (ref.band_inv[0], ref.band_inv[1]))
+        zs[:, led_rows(l), :] = value.reshape(4, rows, 2 * quarter)
+
+    def emit_band(x, l):
+        left = [part[:, led_rows(l), :].reshape(4 * rows, 2 * quarter) for part in (hi, lo)]
+        flipped = dot3(left, (ref.band[0], ref.band[1])).T
+        deep = x.y.shape[2]
+        for pair in range(2):
+            at = slice(pair * lanes, (pair + 1) * lanes)
+            for k, block in enumerate(braid(flipped[:rows, at], flipped[rows:, at])):
+                for q in range(per):
+                    x.stage[l, per * (2 * pair + k) + q] = block[q * deep : (q + 1) * deep]
+        push(x, l)
 
     def tilt(l, here, a, value, sign):
         rc, rs = ref.tilt_r[2 * l, here, :], ref.tilt_r[2 * l + 1, here, :]
@@ -618,43 +626,46 @@
         each_led(stage)
 
     def pupil_columns(x, out, sign):
-        land(x, 0)
-        middle = lanes // 2
-        lane = lax.broadcasted_iota(jnp.int32, x.y.shape[2:], 1)
-        pieces = [[], []]
-        for s in range(0, devs, 2):
-            even, odd = x.y[0, s], x.y[0, s + 1]
-            pieces[0].append(jnp.where(lane < middle, even, pltpu.roll(odd, middle, 1)))
-            pieces[1].append(jnp.where(lane < middle, pltpu.roll(even, middle, 1), odd))
-        field = jnp.concatenate([jnp.concatenate(p, 1) for p in pieces], 0)
-        wide = ref.pupil_in.shape[2] // 2
-        deep = ref.pupil_out.shape[2] // 2
-        cols = x.y.shape[2] // 2
-        both = dot3(split(field), (ref.pupil_in[0], ref.pupil_in[1]))
-        scaled = []
-        for l in range(count):
-            re = slice(2 * l * cols, (2 * l + 1) * cols)
-            im = slice((2 * l + 1) * cols, (2 * l + 2) * cols)
-            yr = both[re, :wide] + both[im, wide:]
-            yi = both[im, :wide] - both[re, wide:]
-            pr, pi = ref.pupil[0], sign * ref.pupil[1]
-            scaled += [yr * pr - yi * pi, yr * pi + yi * pr]
-        both = dot3(split(jnp.concatenate(scaled, 0)), (ref.pupil_out[0], ref.pupil_out[1]))
-        found = []
-        for l in range(count):
-            re = slice(2 * l * cols, (2 * l + 1) * cols)
-            im = slice((2 * l + 1) * cols, (2 * l + 2) * cols)
-            found.append(
-                jnp.concatenate(
-                    [both[re, :deep] - both[im, deep:], both[im, :deep] + both[re, deep:]], 0
-                )
-            )
-        for s in range(0, devs, 2):
-            at = slice(s * middle, s * middle + lanes)
-            first, second = found[0][:, at], found[1][:, at]
-            out.stage[0, s] = jnp.where(lane < middle, first, pltpu.roll(second, middle, 1))
-            out.stage[0, s + 1] = jnp.where(lane < middle, pltpu.roll(first, middle, 1), second)
-        push(out, 0)
+        deep = x.y.shape[2]
+
+        def stage(l):
+            land(x, l)
+            blocks = []
+            for a in range(4):
+                pairs = [braid(x.y[l, s], x.y[l, s + 1]) for s in range(per * a, per * (a + 1), 2)]
+                blocks.append(tuple(jnp.concatenate([pair[k] for pair in pairs], 1) for k in range(2)))
+            mixed = [jnp.concatenate(part, 1) for part in row_spread(blocks, ref.row_twiddle)]
+            z = dot3(split(jnp.concatenate(mixed, 0)), (ref.band[0], ref.band[1]))
+            z = z * ref.shape[0] + sign * (pltpu.roll(z, lanes // 2, 1) * ref.shape[1])
+            y = dot3(split(z), (ref.band_inv[0], ref.band_inv[1]))
+            parts = [(y[j * deep : (j + 1) * deep, :quarter], y[j * deep : (j + 1) * deep, quarter:]) for j in range(4)]
+            for a, (re, im) in enumerate(row_gather(parts, ref.row_twiddle)):
+                for k in range(quarter // lanes):
+                    at = slice(k * lanes, (k + 1) * lanes)
+                    first, second = braid(re[:, at], im[:, at])
+                    out.stage[l, per * a + 2 * k] = first
+                    out.stage[l, per * a + 2 * k + 1] = second
+            push(out, l)
+
+        each_led(stage)
+
+    def shape_pupil():
+        local(ref.pupil, ref.pupil, ref.pupil_got).wait()
+        band, deep = ref.pupil.shape[2], ref.pupil.shape[1]
+        freq = lax.broadcasted_iota(jnp.int32, (band, 4 * lanes), 0)
+        slot = lax.broadcasted_iota(jnp.int32, (band, 4 * lanes), 1)
+        wanted = 4 * lax.rem(slot, lanes // 2) + slot // lanes
+        pick = jnp.where(freq == wanted, 1.0, 0.0).astype(bf16)
+        value, out = ref.pupil[...].reshape(2 * deep, band), 0.0
+        for k in range(3):
+            high = value.astype(bf16)
+            out = out + jnp.dot(high, pick, preferred_element_type=f32)
+            value = value - high.astype(f32)
+        lane = lax.broadcasted_iota(jnp.int32, (deep, lanes), 1)
+        for j in range(4):
+            at = slice(j * lanes, (j + 1) * lanes)
+            ref.shape[0, j * deep : (j + 1) * deep] = out[:deep, at]
+            ref.shape[1, j * deep : (j + 1) * deep] = jnp.where(lane < lanes // 2, -out[deep:, at], out[deep:, at])
 
     def phases(source, target):
         def chunk(base, here, carry):
@@ -697,7 +708,30 @@
             tilts[2 * l + 1] = jnp.sin(angle)[:deep]
 
     pl.semaphore_wait(barrier, everyone - 1)
-    trade_foreign("slab", 0, 1, 2)
+    pieces = (pl.ds(0, share // 2), pl.ds(share // 2, share // 2))
+
+    def piece(source, target, sent, k, device):
+        return away(source, target, sent, ref.piece_got.at[k], device)
+
+    def first_hop(k):
+        at = pieces[k]
+        return piece(
+            sources["slab"].at[0, share:].at[at], ref.slab_relay.at[0, at], semaphore("slab", "_sent", 0), k, neighbour
+        )
+
+    def first_onward(k):
+        at = pieces[k]
+        return away(
+            ref.slab_relay.at[0, at], targets["slab"].at[0, share:].at[at], semaphore("slab", "_sent", 0),
+            semaphore("slab", "_late", 0), across,
+        )
+
+    @pl.when(foreign)
+    def _():
+        direct("slab", 0).start()
+        for k in range(2):
+            first_hop(k).start()
+
     ready("row_twiddle")
     ready("full")
     x0, x1, x2, x3 = port("x0"), port("x1"), port("x2"), port("x3")
@@ -724,11 +758,6 @@
                 ]
         for mask in far_first:
             push_one(x0, 0, mask, span)
-
-    @pl.when(native)
-    def _():
-        traded("slab", 0)
-        enter(0, rows)
 
 
     for name in ("phase", "mask"):
@@ -758,7 +787,15 @@
                 for w in range(2):
                     pupil_copy(jj, w, q).start()
 
-    forward_on("slab", 0)
+
+    @pl.when(native)
+    def _():
+        for k in range(2):
+            first_hop(k).wait_recv()
+            first_onward(k).start()
+        traded("slab", 0)
+        enter(0, rows)
+
     cutoff = size // 2 * (size // 2)
 
     def centred(index):
@@ -782,9 +819,7 @@
                 ref.prop[1, l, j, here, :] = jnp.where(inside, jnp.sin(shift), 0.0)
         return carry
 
-    lax.fori_loop(0, quarter // step // 2, spectrum, 0)
-    forward_on("slab", 1)
-    lax.fori_loop(quarter // step // 2, quarter // step, spectrum, 0)
+    lax.fori_loop(0, quarter // step, spectrum, 0)
 
     @pl.when(foreign)
     def _():
@@ -810,11 +845,12 @@
             ).start()
         else:
             local(counts.stage.at[0, dest], counts.y.at[0, place], counts.got.at[0]).start()
-    forward_on("slab", 2)
     ready("col_twiddle")
     ready("both")
     ready("full_inv")
+    trade_foreign("slab", 1)
     land(x0, 0)
+    forward_on("slab", 1)
     spread(x0, 0)
 
     def keep_spectrum(j, z):
@@ -828,6 +864,7 @@
         col_inverse(x1, l)
 
     each_led(first)
+    trade_foreign("slab", 2)
     land(counts, 0)
     count_sum = jnp.sum(jnp.sum(counts.y[0], 0), 1, keepdims=True)
     area = spec.area
@@ -853,6 +890,7 @@
     each_chunk(gather_counts)
     for k in range(spec.sets):
         trade_native("lit", k)
+    trade_foreign("lit", 0)
     slab_phases(1)
 
     def forward(l):
@@ -875,11 +913,17 @@
         emit_full(x2, l, l)
 
     each_led(forward)
-    trade_foreign("lit", 0)
+    forward_on("slab", 2)
+    forward_on("lit", 0)
+    trade_foreign("lit", 1)
     columns(x2, x3, 1.0)
-    trade_foreign("lit", *range(1, spec.sets))
-    forward_on("lit", 0)
+    trade_foreign("lit", *range(2, spec.sets))
+    forward_on("lit", 1)
     slab_phases(2)
+    b0, b1, b2, b3, sums = port("b0"), port("b1"), port("b2"), port("b3"), port("sums")
+    ready("band")
+    ready("band_inv")
+    shape_pupil()
 
     def forward_band(l):
         land(x3, l)
@@ -898,21 +942,19 @@
             return carry
 
         each_chunk(chunk)
+        emit_band(b0, l)
 
     each_led(forward_band)
-    forward_on("lit", *range(1, spec.sets))
-    b0, b1, b2, b3, sums = port("b0"), port("b1"), port("b2"), port("b3"), port("sums")
-    ready("band")
-    emit_band(b0)
-    ready("pupil_in")
-    ready("pupil_out")
-    local(ref.pupil, ref.pupil, ref.pupil_got).wait()
+    forward_on("lit", *range(2, spec.sets))
     pupil_columns(b0, b1, 1.0)
+
+    def camera(l):
+        land(b1, l)
+        inverse_band(b1, l)
+
+    each_led(camera)
     for k in range(spec.sets):
         traded("lit", k)
-    ready("band_inv")
-    land(b1, 0)
-    inverse_band(b1)
 
     def measure(base, here, carry):
         fields = [gathered(l, base) for l in range(count)]
@@ -985,14 +1027,15 @@
         return carry
 
     each_chunk(weigh)
-    emit_band(b2)
+    each_led(lambda l: emit_band(b2, l))
     pupil_columns(b2, b3, -1.0)
-    land(b3, 0)
-    inverse_band(b3)
     y3, y2, y1, y0 = port("y3"), port("y2"), port("y1"), port("y0")
     ref.grad[...] = jnp.zeros(ref.grad.shape, f32)
 
     def back_band(l):
+        land(b3, l)
+        inverse_band(b3, l)
+
         def chunk(base, here, carry):
             fields, at, blocks = gathered(l, base), spot(l, base), []
             for a, c in enumerate(cut):
@@ -1077,7 +1120,7 @@
     final.start()
 
     for x, slots in (
-        (x0, 1), (x1, count), (x2, count), (x3, count), (b0, 1), (b1, 1), (b2, 1), (b3, 1),
+        (x0, 1), (x1, count), (x2, count), (x3, count), (b0, count), (b1, count), (b2, count), (b3, count),
         (sums, 1), (counts, 1), (y3, count), (y2, count), (y1, count), (y0, 1),
     ):
         drain(x, slots)
@@ -1109,7 +1152,7 @@
     quarter, cols, per = size // 4, size // devs, devs // 4
     band = 2 * pupil_radius
     band_cols = band // devs
-    rt = row_tables(size, cols, band_cols)
+    rt = row_tables(size, cols, band // 4)
     ct = col_tables(size)
     sets = 2**count - 1
     stat_rows = count + count * (count + 1) // 2 + count * 2 ** (count - 1)
@@ -1117,7 +1160,7 @@
     loads = dict(
         row_twiddle=rt.twiddle, full=rt.full,
         col_twiddle=jnp.asarray(ct.twiddle), both=jnp.asarray(ct.both), full_inv=rt.full_inv, band=rt.band,
-        pupil_in=jnp.asarray(ct.band), pupil_out=jnp.asarray(ct.band_inv), band_inv=rt.band_inv, measured=measured,
+        band_inv=rt.band_inv, measured=measured,
     )
     inputs = {name + "_hbm": value for name, value in loads.items()}
     inputs |= dict(phase_hbm=pupil_phase, mask_hbm=pupil_mask, slab_hbm=slab_phase, freq=led_freq, code=led_code.T)
@@ -1130,7 +1173,7 @@
     scratch |= dict(
         slab=vmem(slab_phase.shape, f32), lit=vmem((sets, rows, size), f32), lit_own=vmem((sets, rows, size), f32),
         phase=vmem((2, rows, pupil_radius), f32), mask=vmem((2, rows, pupil_radius), jnp.int32),
-        phase_sem=dma((2,)), mask_sem=dma((2,)), own=vmem((4, 2, rows // 4, band), f32), pupil=vmem((2, band_cols, band), f32),
+        phase_sem=dma((2,)), mask_sem=dma((2,)), own=vmem((4, 2, rows // 4, band), f32), pupil=vmem((2, band_cols, band), f32), shape=vmem((2, 4 * band_cols, lanes), f32),
         tilt_c=vmem((2 * count, 1, size), f32), tilt_r=vmem((2 * count, rows, lanes), f32),
         prop=vmem((2, count, 4, quarter, lanes), f32), tr=vmem((3, 2, rows, size), f32),
         passed1=vmem((2, total, size), f32), passed2=vmem((2, total, size), f32),
@@ -1141,15 +1184,15 @@
         dhi=vmem((quarter, 4 * lanes), bf16), dlo=vmem((quarter, 4 * lanes), bf16),
         cz=vmem((4, quarter, lanes), f32), cs=vmem((4, quarter, lanes), f32),
         loads=dma((len(loads) + 1,)),
-        pupil_sent=dma((4,)), pupil_got=dma,
+        pupil_sent=dma((4,)), pupil_got=dma, piece_got=dma((2,)),
     )
     for name, blocks in (("slab", 3), ("lit", sets), ("grad", 2)):
         scratch[name + "_relay"] = vmem((blocks, rows // 2, size), f32)
         for kind in ("_sent", "_got", "_late", "_via"):
             scratch[name + kind] = dma((blocks,))
-    block, narrow = (devs, rows, lanes), (devs, 2 * band_cols, total)
+    block, narrow = (devs, rows, lanes), (devs, band_cols, lanes)
     ports = dict(x0=(1, block), x1=(count, block), x2=(count, block), x3=(count, block))
-    ports |= dict(b0=(1, narrow), b1=(1, narrow), b2=(1, narrow), b3=(1, narrow))
+    ports |= dict(b0=(count, narrow), b1=(count, narrow), b2=(count, narrow), b3=(count, narrow))
     ports |= dict(sums=(1, (devs, -(-stat_rows // 8) * 8, lanes)))
     ports |= dict(counts=(1, (devs, -(-patterns // 8) * 8, lanes)))
     ports |= dict(y3=(count, block), y2=(count, block), y1=(count, block), y0=(1, block))

time: 182 us -> 170 us (0.934); the launches traced: 179 us -> 169 us
  Pallas kernels: 177 us -> 167 us
    pallas_call x1, Pallas kernels: 177 us -> 167 us  [body(): pl.pallas_call(functools.partial(whole_kernel, spec), out_shape=jax.Shape...]
where the time goes in v3:
time: 170 us; the launch traced here: 169 us
  Pallas kernels  167 us (98%)
  local copies, waits for them, and re-layouts  2.09 us (1%)
    pallas_call x1, Pallas kernels, body(): pl.pallas_call(functools.partial(whole_kernel, spec), out_shape=jax.Shape...  167 us

profile of v3, /device:TPU:4, one launch (start us, length us, event | category | flops | bytes accessed | tf_op | source)
XLA Modules:
  0.0 169.3 jit_solution(13409666267267661819)
XLA Ops:
  0.0 167.2 %whole.1 = f32[3,64,1024]{2,1,0:T(8,128)} custom-call(f32[8,256]{1,0:T(8,128)} %constant.18.clone.refs_0_, bf16[2,512,512]{2,1,0:T(8,128)(2,1)} %constant.14.clone.refs_1_, f32[2,3,256,128]{3,2,1,0:T(8,128)} %constant.19.clone.refs_2_, bf16[2,512,256]{2,1,0:T(8,128)(2,1)} %constant.20.clone.refs_3_, bf16[2,512,512]{2,1,0:T(8,128)(2,1)} %constant.15.clone.refs_4_, ...), custom_call_target="tpu_custom_call" | custom-call | tf_op jit(solution)/shard_map/whole/pallas_call | solution.py:1211
  167.2 2.1 %copy.15 = f32[3,64,1024]{2,1,0:T(8,128)} copy(f32[3,64,1024]{2,1,0:T(8,128)} %whole.1) | data formatting | bytes 1572864

commit v4 on v3

--- a/solution.py
+++ b/solution.py
@@ -636,7 +636,12 @@
                 blocks.append(tuple(jnp.concatenate([pair[k] for pair in pairs], 1) for k in range(2)))
             mixed = [jnp.concatenate(part, 1) for part in row_spread(blocks, ref.row_twiddle)]
             z = dot3(split(jnp.concatenate(mixed, 0)), (ref.band[0], ref.band[1]))
+            if sign < 0.0:
+                z = z - ref.pulled[l] * ref.spectrum[l]
             z = z * ref.shape[0] + sign * (pltpu.roll(z, lanes // 2, 1) * ref.shape[1])
+            if sign > 0.0:
+                ref.spectrum[l] = z
+                ref.energy[l] = jnp.sum(z * z, 0, keepdims=True)
             y = dot3(split(z), (ref.band_inv[0], ref.band_inv[1]))
             parts = [(y[j * deep : (j + 1) * deep, :quarter], y[j * deep : (j + 1) * deep, quarter:]) for j in range(4)]
             for a, (re, im) in enumerate(row_gather(parts, ref.row_twiddle)):
@@ -947,6 +952,19 @@
     each_led(forward_band)
     forward_on("lit", *range(2, spec.sets))
     pupil_columns(b0, b1, 1.0)
+    means = port("means")
+
+    def announce(x, lines):
+        lines = jnp.concatenate(lines + [jnp.zeros((x.stage.shape[2] - len(lines), lanes), f32)], 0)
+        for d in range(devs):
+            x.stage[0, d] = lines
+        push(x, 0)
+
+    def heard(x):
+        land(x, 0)
+        return jnp.sum(jnp.sum(x.y[0], 0), 1, keepdims=True)
+
+    announce(means, [ref.energy[l] for l in range(count)])
 
     def camera(l):
         land(b1, l)
@@ -956,78 +974,55 @@
     for k in range(spec.sets):
         traded("lit", k)
 
-    def measure(base, here, carry):
+    added = heard(means)
+    pairs = [(l, m) for l in range(count) for m in range(l, count)]
+    inverse_mean, number = [], []
+    for k, leds in enumerate(lit_sets):
+        members = sum(member_of[k])
+        inverse = jnp.where(members > 0.0, area / sum(added[l : l + 1] for l in leds), 0.0)
+        inverse_mean.append(inverse)
+        number.append(members * inverse)
+
+    def weigh(base, here, carry):
         fields = [gathered(l, base) for l in range(count)]
-        adds = [0.0] * spec.stat_rows
+        adds, outgoing = [0.0] * spec.stat_rows, [[] for _ in range(count)]
         for a, c in enumerate(cut):
-            power = []
-            for l in range(count):
-                at = spot(l, base)
-                re, im = fields[l][a]
-                ref.camera[0, at, c] = re
-                ref.camera[1, at, c] = im
-                power.append(re * re + im * im)
-            values = list(power)
-            for l in range(count):
-                for m in range(l, count):
-                    values.append(power[l] * power[m])
+            power = [fields[l][a][0] * fields[l][a][0] + fields[l][a][1] * fields[l][a][1] for l in range(count)]
+            values = [power[l] * power[m] for l, m in pairs]
+            weight = [0.0] * count
             for k, leds in enumerate(lit_sets):
                 seen = ref.lit[k, here, c]
                 values += [seen * power[l] for l in leds]
-            for k, value in enumerate(values):
-                adds[k] = adds[k] + fold(value)
-        return tuple(x + y for x, y in zip(carry, adds))
-
-    stats = each_chunk(measure, tuple(jnp.zeros((8, lanes), f32) for _ in range(spec.stat_rows)))
-    packed = [jnp.sum(line, 0, keepdims=True) for line in stats]
-    packed.append(jnp.zeros((sums.stage.shape[2] - len(packed), lanes), f32))
-    packed = jnp.concatenate(packed, 0)
-    for d in range(devs):
-        sums.stage[0, d] = packed
-    push(sums, 0)
-    land(sums, 0)
-    added = jnp.sum(jnp.sum(sums.y[0], 0), 1, keepdims=True)
-    pairs = [(l, m) for l in range(count) for m in range(l, count)]
-    cross_row = count + len(pairs)
-    inverse_mean, number, couple = [], [], []
-    for k, leds in enumerate(lit_sets):
-        mean = sum(added[l : l + 1] for l in leds) / area
-        members = sum(member_of[k])
-        inverse = jnp.where(members > 0.0, 1.0 / mean, 0.0)
-        square = 0.0
-        for at, (l, m) in enumerate(pairs):
-            if l in leds and m in leds:
-                square = square + (1.0 if l == m else 2.0) * added[count + at : count + at + 1]
-        cross = sum(added[cross_row + i : cross_row + i + 1] for i in range(len(leds)))
-        cross_row += len(leds)
-        inverse_mean.append(inverse)
-        number.append(members * inverse)
-        couple.append((members * square * inverse * inverse - cross * inverse) / area)
-
-    def weigh(base, here, carry):
-        outgoing = [[] for _ in range(count)]
-        for a, c in enumerate(cut):
-            camera, power = [], []
-            for l in range(count):
-                at = spot(l, base)
-                re, im = ref.camera[0, at, c], ref.camera[1, at, c]
-                camera.append((re, im))
-                power.append(re * re + im * im)
-            weight = [0.0] * count
-            for k, leds in enumerate(lit_sets):
-                lit = sum(power[l] for l in leds)
-                pull = (lit * number[k] - ref.lit[k, here, c] - couple[k]) * inverse_mean[k]
+                pull = (sum(power[l] for l in leds) * number[k] - seen) * inverse_mean[k]
                 for l in leds:
                     weight[l] = weight[l] + pull
             for l in range(count):
                 scale = 2.0 * weight[l]
-                outgoing[l].append((scale * camera[l][0], scale * camera[l][1]))
+                outgoing[l].append((scale * fields[l][a][0], scale * fields[l][a][1]))
+            for k, value in enumerate(values):
+                adds[k] = adds[k] + fold(value)
         for l in range(count):
             scattered(l, base, outgoing[l])
-        return carry
-
-    each_chunk(weigh)
+        return tuple(x + y for x, y in zip(carry, adds))
+
+    stats = each_chunk(weigh, tuple(jnp.zeros((8, lanes), f32) for _ in range(spec.stat_rows)))
+    announce(sums, [jnp.sum(line, 0, keepdims=True) for line in stats])
     each_led(lambda l: emit_band(b2, l))
+    added = heard(sums)
+    pulls = [0.0] * count
+    cross_row = len(pairs)
+    for k, leds in enumerate(lit_sets):
+        square = 0.0
+        for at, (l, m) in enumerate(pairs):
+            if l in leds and m in leds:
+                square = square + (1.0 if l == m else 2.0) * added[at : at + 1]
+        cross = sum(added[cross_row + i : cross_row + i + 1] for i in range(len(leds)))
+        cross_row += len(leds)
+        couple = (number[k] * square * inverse_mean[k] - cross * inverse_mean[k]) / area
+        for l in leds:
+            pulls[l] = pulls[l] + couple * inverse_mean[k]
+    for l in range(count):
+        ref.pulled[l] = jnp.broadcast_to(2.0 * pulls[l], (1, lanes))
     pupil_columns(b2, b3, -1.0)
     y3, y2, y1, y0 = port("y3"), port("y2"), port("y1"), port("y0")
     ref.grad[...] = jnp.zeros(ref.grad.shape, f32)
@@ -1121,7 +1116,7 @@
 
     for x, slots in (
         (x0, 1), (x1, count), (x2, count), (x3, count), (b0, count), (b1, count), (b2, count), (b3, count),
-        (sums, 1), (counts, 1), (y3, count), (y2, count), (y1, count), (y0, 1),
+        (sums, 1), (means, 1), (counts, 1), (y3, count), (y2, count), (y1, count), (y0, 1),
     ):
         drain(x, slots)
     for q in range(per):
@@ -1155,7 +1150,7 @@
     rt = row_tables(size, cols, band // 4)
     ct = col_tables(size)
     sets = 2**count - 1
-    stat_rows = count + count * (count + 1) // 2 + count * 2 ** (count - 1)
+    stat_rows = count * (count + 1) // 2 + count * 2 ** (count - 1)
     owners = [(q - pupil_radius // cols) % devs for q in range(per)]
     loads = dict(
         row_twiddle=rt.twiddle, full=rt.full,
@@ -1177,7 +1172,8 @@
         tilt_c=vmem((2 * count, 1, size), f32), tilt_r=vmem((2 * count, rows, lanes), f32),
         prop=vmem((2, count, 4, quarter, lanes), f32), tr=vmem((3, 2, rows, size), f32),
         passed1=vmem((2, total, size), f32), passed2=vmem((2, total, size), f32),
-        camera=vmem((2, total, size), f32), grad=vmem((2, rows, size), f32), grad0=vmem((rows, size), f32),
+        spectrum=vmem((count, 4 * band_cols, lanes), f32), energy=vmem((count, 1, lanes), f32),
+        pulled=vmem((count, 1, lanes), f32), grad=vmem((2, rows, size), f32), grad0=vmem((rows, size), f32),
         hi=vmem((4, total, wide), bf16), lo=vmem((4, total, wide), bf16), zs=vmem((4, total, wide), f32),
         ghi=vmem((4 * rows, wide), bf16), glo=vmem((4 * rows, wide), bf16),
         chi=vmem((quarter, 4 * lanes), bf16), clo=vmem((quarter, 4 * lanes), bf16),
@@ -1194,6 +1190,7 @@
     ports = dict(x0=(1, block), x1=(count, block), x2=(count, block), x3=(count, block))
     ports |= dict(b0=(count, narrow), b1=(count, narrow), b2=(count, narrow), b3=(count, narrow))
     ports |= dict(sums=(1, (devs, -(-stat_rows // 8) * 8, lanes)))
+    ports |= dict(means=(1, (devs, -(-count // 8) * 8, lanes)))
     ports |= dict(counts=(1, (devs, -(-patterns // 8) * 8, lanes)))
     ports |= dict(y3=(count, block), y2=(count, block), y1=(count, block), y0=(1, block))
     for name, (slots, shape) in ports.items():

time: 170 us -> 168 us (0.988)
  no operation moved by 1% of the time
where the time goes in v4:
time: 168 us
  Pallas kernels  166 us (99%)
  local copies, waits for them, and re-layouts  2.09 us (1%)
    pallas_call x1, Pallas kernels, body(): pl.pallas_call(functools.partial(whole_kernel, spec), out_shape=jax.Shape...  166 us

profile of v4, /device:TPU:4, one launch (start us, length us, event | category | flops | bytes accessed | tf_op | source)
XLA Modules:
  0.0 168.2 jit_solution(3166935588006591600)
XLA Ops:
  0.0 166.1 %whole.1 = f32[3,64,1024]{2,1,0:T(8,128)} custom-call(f32[8,256]{1,0:T(8,128)} %constant.18.clone.refs_0_, bf16[2,512,512]{2,1,0:T(8,128)(2,1)} %constant.14.clone.refs_1_, f32[2,3,256,128]{3,2,1,0:T(8,128)} %constant.19.clone.refs_2_, bf16[2,512,256]{2,1,0:T(8,128)(2,1)} %constant.20.clone.refs_3_, bf16[2,512,512]{2,1,0:T(8,128)(2,1)} %constant.15.clone.refs_4_, ...), custom_call_target="tpu_custom_call" | custom-call | tf_op jit(solution)/shard_map/whole/pallas_call | solution.py:1208
  166.1 2.1 %copy.15 = f32[3,64,1024]{2,1,0:T(8,128)} copy(f32[3,64,1024]{2,1,0:T(8,128)} %whole.1) | data formatting | bytes 1572864

commit v5 on v4

--- a/solution.py
+++ b/solution.py
@@ -513,12 +513,14 @@
         zs[:, led_rows(l), :] = value.reshape(4, rows, 2 * quarter)
 
     def emit_full(x, slot, l):
-        left = [part[:, led_rows(l), :].reshape(4 * rows, 2 * quarter) for part in (hi, lo)]
-        value = dot3(left, (ref.full[0], ref.full[1]))
-        for j in range(4):
+        home = me // per
+        for far in (3, 1, 2, 0):
+            j = flip(home, far)
+            value = dot3((hi[j, led_rows(l), :], lo[j, led_rows(l), :]), (ref.full[0], ref.full[1]))
             for q in range(per):
-                x.stage[slot, per * j + q] = value[j * rows : (j + 1) * rows, q * lanes : (q + 1) * lanes]
-        push(x, slot)
+                x.stage[slot, per * j + q] = value[:, q * lanes : (q + 1) * lanes]
+            for bits in (3, 2, 1, 0):
+                push_one(x, slot, per * far + bits)
 
     def braid(first, second):
         middle = lanes // 2
@@ -1044,12 +1046,13 @@
 
         each_chunk(chunk)
 
+        emit_full(y3, l, l)
+
         @pl.when(l == count - 1)
         def _():
             trade_native("grad", 1)
             trade_foreign("grad", 1)
 
-        emit_full(y3, l, l)
 
     each_led(back_band)
     columns(y3, y2, -1.0)

time: 168 us -> 166 us (0.988)
  Pallas kernels: 166 us -> 163 us
    pallas_call x1, Pallas kernels: 166 us -> 163 us  [body(): pl.pallas_call(functools.partial(whole_kernel, spec), out_shape=jax.Shape...]
where the time goes in v5:
time: 166 us; the launch traced here: 165 us
  Pallas kernels  163 us (98%)
  local copies, waits for them, and re-layouts  2.09 us (1%)
    pallas_call x1, Pallas kernels, body(): pl.pallas_call(functools.partial(whole_kernel, spec), out_shape=jax.Shape...  163 us

profile of v5, /device:TPU:4, one launch (start us, length us, event | category | flops | bytes accessed | tf_op | source)
XLA Modules:
  0.0 165.1 jit_solution(4324798903725968476)
XLA Ops:
  0.0 163.0 %whole.1 = f32[3,64,1024]{2,1,0:T(8,128)} custom-call(f32[8,256]{1,0:T(8,128)} %constant.18.clone.refs_0_, bf16[2,512,512]{2,1,0:T(8,128)(2,1)} %constant.14.clone.refs_1_, f32[2,3,256,128]{3,2,1,0:T(8,128)} %constant.19.clone.refs_2_, bf16[2,512,256]{2,1,0:T(8,128)(2,1)} %constant.20.clone.refs_3_, bf16[2,512,512]{2,1,0:T(8,128)(2,1)} %constant.15.clone.refs_4_, ...), custom_call_target="tpu_custom_call" | custom-call | tf_op jit(solution)/shard_map/whole/pallas_call | solution.py:1211
  163.0 2.1 %copy.15 = f32[3,64,1024]{2,1,0:T(8,128)} copy(f32[3,64,1024]{2,1,0:T(8,128)} %whole.1) | data formatting | bytes 1572864
